TPU v7x, 32 devices: a whole 2x2x4 slice. The times are simulated.
32 devices in a mesh: grp: 2 (over y), bin: 4 (over z), slab: 4 (over x, core).
Axes of the slice: x: 2, y: 2, z: 4, core: 2. Of those that a mesh axis runs over, the one named last changes fastest.
Arguments:
- density: bfloat16 [512, 256, 256], P('grp', 'slab'), parts along dimension 0, may hold values from -6 to 6
- images: bfloat16 [512, 128, 128], P(('grp', 'bin', 'slab')), parts along dimension 0, may hold values from -6 to 6
- image_bin: int32 [512, 1], P(('grp', 'bin', 'slab')), parts along dimension 0, may hold values from 0 to 3; in each aligned block of 16 rows (0 to 15, 16 to 31, ...) at most 4 rows name the same one
- image_pose: int32 [512], P(('grp', 'bin', 'slab')), parts along dimension 0, may hold values from 0 to 7
- image_class: int32 [512], P(('grp', 'bin', 'slab')), parts along dimension 0, may hold values from 0 to 15
- defocus: float32 [32], P('grp'), parts along dimension 0, may hold values from 1 to 3
- pose_offset: float32 [8, 8], P('grp'), parts along dimension 0, may hold values from 0 to 1
- step_sizes: float32 [2], replicated, may hold values from 0.2 to 0.8
Outputs:
- gradient: float32 [512, 256, 256], P(('grp', 'bin'), 'slab'), parts along dimension 0
- refined: float32 [512, 256, 256], P(('grp', 'bin'), 'slab'), parts along dimension 0
There are 2 independent parts, one for each index of `grp`. A program takes and returns all parts, laid end to end along the dimension named above; an argument that names none is the same for every part. Nothing has to cross between parts.
Inputs may be any that keep to these rules, and one draw needn't show every extreme that they name: `image_bin`: the images of one device name each bin at most 4 times, a bound that some block reaches.
All inputs are finite; a program needn't handle non-finite values.
Results may differ from a plain program's by a relative error of at most 0.0032.
Values may be sent and summed in bfloat16 or wider, within the bound.
No kernel may reach another device: no remote copies, remote signals or barrier semaphores. Data moves between devices by JAX's collectives and lax.ppermute only.
A program may use at most 256 MiB of HBM per device.

v0:
```python
import functools
import math

import jax
import jax.numpy as jnp
import numpy as np
from jax import lax
from jax.experimental import pallas as pl
from jax.experimental.pallas import tpu as pltpu
from jax.sharding import PartitionSpec as P


AMP_CONTRAST = 0.1
PHASE_RATE = 60.0
BLOCK = 16
WINDOW = 16
LANES = 128
SMEM = pltpu.SMEM


def vmem():
    return pl.BlockSpec(memory_space=pltpu.VMEM)


def smem():
    return pl.BlockSpec(memory_space=SMEM)


def pool_table(image_side, map_side):
    row_index = np.arange(image_side)[:, None]
    col_index = np.arange(map_side)[None, :]
    return 0.5 * np.maximum(0.0, 1.0 - np.abs(col_index - 2.0 * row_index - 0.5) / 2.0)


def hartley_table(image_side):
    index_row = np.arange(image_side)
    phase_index = index_row[:, None] * index_row[None, :] % image_side
    angle_table = 2.0 * math.pi / image_side * phase_index
    table = (np.cos(angle_table) + np.sin(angle_table)) / math.sqrt(image_side)
    high = table.astype(jnp.bfloat16)
    low = (table - high.astype(np.float64)).astype(jnp.bfloat16)
    return jnp.asarray(np.concatenate([high, low], axis=1))


def fill_ctf(ctf, defocus):
    classes, side, _ = ctf.shape
    row = lax.broadcasted_iota(jnp.int32, (classes, side), 0)
    lane = lax.broadcasted_iota(jnp.int32, (classes, side), 1)
    value = jnp.zeros((classes, side), jnp.float32)
    for c in range(classes):
        value = jnp.where(row == c, defocus[c], value)
    frequency = jnp.where(lane < side // 2, lane, lane - side).astype(jnp.float32) / side
    part = PHASE_RATE * value * (frequency * frequency)
    shifted = part + math.asin(AMP_CONTRAST)
    across = (jnp.cos(part), jnp.sin(part))
    down = jnp.concatenate(
        [
            jnp.sin(shifted),
            jnp.cos(shifted),
            jnp.zeros((side - 2 * classes, side), jnp.float32),
        ],
        axis=0,
    ).T
    for c in range(classes):
        ctf[c] = -(
            down[:, c : c + 1] * across[0][c : c + 1]
            + down[:, classes + c : classes + c + 1] * across[1][c : c + 1]
        )


def block_lines(theta, y_low, z_low, side, map_side):
    middle = map_side / 2.0
    scale = 0.25 / math.sqrt(map_side)
    cosine, sine = jnp.cos(theta), jnp.sin(theta)
    y_part = (y_low.astype(jnp.float32) + (0.5 - middle)) * cosine
    z_part = (z_low.astype(jnp.float32) + (0.5 - middle)) * sine
    least = (
        y_part
        + jnp.minimum(0.0, (BLOCK - 1.0) * cosine)
        + z_part
        + jnp.minimum(0.0, (BLOCK - 1.0) * sine)
    )
    column = jnp.floor((least + (middle - 3.0)) * 0.5).astype(jnp.int32)
    start = jnp.clip(column, 0, side - WINDOW)
    offset = scale * (y_part + z_part - (2.0 * start.astype(jnp.float32) + (1.0 - middle)))
    return cosine * scale, sine * scale, start, offset


def geometry_kernel(
    sizes, offsets, own_cos, own_sin, own_start, own_offset, cosine, sine, start, offset,
    wide, lanes
):
    map_side, side, depth, row_share, bins, chips, owned = sizes
    here, slab = lax.axis_index("bin"), lax.axis_index("slab")
    chip, core = slab // 2, lax.rem(slab, 2)
    first_plane = (chip * 2 + core) * depth
    plane_blocks = depth // BLOCK

    def turn(away, place):
        across, ahead, beyond = away
        bin_at = lax.rem(here + beyond, bins)
        owner = lax.rem(chip + ahead, chips) * 2 + lax.rem(core + across, 2)
        return bin_at.astype(jnp.float32) + offsets[bin_at, owner * owned + place]

    def listed(beyonds):
        return [
            turn((across, ahead, beyond), place)
            for across in range(2)
            for ahead in range(chips)
            for beyond in range(beyonds)
            for place in range(owned)
        ]

    def spread(values, index, shape):
        theta = jnp.zeros(shape, jnp.float32)
        for k, value in enumerate(values):
            theta = jnp.where(index == k, value, theta)
        return math.pi * theta / bins

    def fill(outs, values, first_row):
        shape = outs[0].shape
        row = lax.broadcasted_iota(jnp.int32, shape, 0)
        block = lax.broadcasted_iota(jnp.int32, shape, 1)
        theta = spread(values, row, shape)
        found = block_lines(
            theta,
            first_row + block // plane_blocks * BLOCK,
            first_plane + block % plane_blocks * BLOCK,
            side,
            map_side,
        )
        for out, value in zip(outs, found):
            out[...] = value

    first_row = here * row_share
    values = listed(bins)
    fill((own_cos, own_sin, own_start, own_offset), listed(1), 0)
    fill((cosine, sine, start, offset), values, first_row)
    shape = lanes.shape
    block = lax.broadcasted_iota(jnp.int32, shape, 0)
    lane = lax.broadcasted_iota(jnp.int32, shape, 1)
    along_y, along_z, _, offset_wide = block_lines(
        spread(values, lane // WINDOW, shape),
        first_row + block // plane_blocks * BLOCK,
        first_plane + block % plane_blocks * BLOCK,
        side,
        map_side,
    )
    peak = 0.5 / math.sqrt(map_side)
    lanes[...] = offset_wide - peak * (lane % WINDOW).astype(jnp.float32)
    wide[0:1, :] = along_y[0:1]
    wide[1:2, :] = along_z[0:1]


def make_geometry(pose_offset, map_side, side, depth, row_share, chips, owned):
    bins, pose_count = pose_offset.shape
    poses = bins * pose_count

    def tables(count, blocks):
        shape = (count, -(-blocks // LANES) * LANES)
        return [jax.ShapeDtypeStruct(shape, t) for t in (jnp.float32,) * 2] + [
            jax.ShapeDtypeStruct(shape, jnp.int32),
            jax.ShapeDtypeStruct(shape, jnp.float32),
        ]

    plane_blocks = depth // BLOCK
    blocks = row_share // BLOCK * plane_blocks
    shapes = (
        tables(pose_count, map_side // BLOCK * plane_blocks)
        + tables(poses, blocks)
        + [
            jax.ShapeDtypeStruct((2, poses * WINDOW), jnp.float32),
            jax.ShapeDtypeStruct((blocks, poses * WINDOW), jnp.float32),
        ]
    )
    sizes = (map_side, side, depth, row_share, bins, chips, owned)
    out = pl.pallas_call(
        functools.partial(geometry_kernel, sizes),
        in_specs=[smem()],
        out_specs=[vmem()] * len(shapes),
        out_shape=shapes,
        name="geometry",
    )(pose_offset)
    return out[:4], out[4:8], out[8:]


def fill_windows(w_ref, geo, block, poses, map_side):
    lane = lax.broadcasted_iota(jnp.int32, (8, BLOCK * BLOCK), 1)
    row = lax.broadcasted_iota(jnp.int32, (8, BLOCK * BLOCK), 0).astype(jnp.float32)
    y_local = (lane // BLOCK).astype(jnp.float32)
    z_local = (lane % BLOCK).astype(jnp.float32)
    peak = 0.5 / math.sqrt(map_side)
    rows = [peak * (row + 8.0 * k) for k in range(WINDOW // 8)]
    cosine, sine, _, offset = geo
    for pose in range(poses):
        line = y_local * cosine[pose, 0] + z_local * sine[pose, 0] + offset[pose, block]
        parts = [jnp.maximum(0.0, peak - jnp.abs(line - r)) for r in rows]
        w_ref[pose * WINDOW : (pose + 1) * WINDOW, :] = jnp.concatenate(parts, axis=0).astype(
            jnp.bfloat16
        )


def fill_turned(t_ref, wide, lanes, block, map_side):
    peak = 0.5 / math.sqrt(map_side)
    local = lax.broadcasted_iota(jnp.int32, (BLOCK, LANES), 0).astype(jnp.float32)
    offset = lanes[pl.ds(block, 1), :]
    for at in range(0, wide.shape[1], LANES):
        span = slice(at, at + LANES)
        along_z = local * wide[1:2, span] + offset[:, span]
        along_y = wide[0:1, span]
        for y in range(BLOCK):
            line = along_z + float(y) * along_y
            t_ref[y * BLOCK : (y + 1) * BLOCK, span] = jnp.maximum(
                0.0, peak - jnp.abs(line)
            ).astype(jnp.bfloat16)


def windows_kernel(poses, map_side, cosine, sine, start, offset, windows):
    count = windows.shape[0]
    for k in range(count):
        index = pl.program_id(0) * count + k
        fill_windows(windows.at[k], (cosine, sine, start, offset), index, poses, map_side)


def turned_kernel(map_side, wide, lanes, turned):
    count = turned.shape[0]
    for k in range(count):
        index = pl.program_id(0) * count + k
        fill_turned(turned.at[k], wide, lanes, index, map_side)


def table_call(kernel, blocks, shape, operands, specs):
    count = math.gcd(blocks, 4)
    return pl.pallas_call(
        kernel,
        grid=(blocks // count,),
        in_specs=specs,
        out_specs=pl.BlockSpec((count, *shape), lambda i: (i, 0, 0)),
        out_shape=jax.ShapeDtypeStruct((blocks, *shape), jnp.bfloat16),
    )(*operands)


def window_table(geo, blocks, poses, map_side):
    return table_call(
        functools.partial(windows_kernel, poses, map_side), blocks,
        (poses * WINDOW, BLOCK * BLOCK), geo, [smem()] * 4,
    )


def turned_table(wide_geo, blocks, poses, map_side):
    return table_call(
        functools.partial(turned_kernel, map_side), blocks,
        (BLOCK * BLOCK, poses * WINDOW), wide_geo, [vmem()] * 2,
    )


def add_projection(outs, prod, start, block, poses):
    share = poses // len(outs)
    for first in range(0, poses, 8):
        group = range(first, min(first + 8, poses))
        places = [
            (outs[pose // share], pose % share, pl.ds(start[pose, block], WINDOW))
            for pose in group
        ]
        values = [out[at, rows, :] for out, at, rows in places]
        for pose, value, (out, at, rows) in zip(group, values, places):
            out[at, rows, :] = value + prod[pose * WINDOW : (pose + 1) * WINDOW]


def first_projection_kernel(
    map_side, poses, cosine, sine, start, offset, dens, pool_t, keep, send, fold_ref, w_ref
):
    step = pl.program_id(0)
    geo = (cosine, sine, start, offset)

    @pl.when(step == 0)
    def _():
        keep[...] = jnp.zeros_like(keep)
        send[...] = jnp.zeros_like(send)

    height, depth, _ = dens.shape
    side = pool_t.shape[1]
    folded = jnp.dot(
        dens[...].reshape(height * depth, map_side), pool_t[...], preferred_element_type=jnp.float32
    )
    fold_ref[...] = folded.astype(jnp.bfloat16).reshape(height, depth, side)
    count = height * depth // (BLOCK * BLOCK)
    for k in range(count):
        row, plane = k // (depth // BLOCK) * BLOCK, k % (depth // BLOCK) * BLOCK
        weights = w_ref.at[k]
        fill_windows(weights, geo, step * count + k, poses, map_side)
        pixels = fold_ref[row : row + BLOCK, plane : plane + BLOCK, :].reshape(-1, side)
        prod = jnp.dot(weights[...], pixels, preferred_element_type=jnp.float32)
        add_projection((keep, send), prod, start, step * count + k, poses)


def first_projection(density, pool_t, geo, poses):
    map_side, depth, _ = density.shape
    side = pool_t.shape[1]
    height = 2 * BLOCK
    half = jax.ShapeDtypeStruct((poses // 2, side, side), jnp.float32)
    return pl.pallas_call(
        functools.partial(first_projection_kernel, map_side, poses),
        grid=(map_side // height,),
        in_specs=[smem(), smem(), smem(), smem(),
                  pl.BlockSpec((height, depth, map_side), lambda i: (i, 0, 0)),
                  vmem()],
        out_specs=[vmem(), vmem(), pl.BlockSpec((height, depth, side), lambda i: (i, 0, 0))],
        out_shape=[half, half, jax.ShapeDtypeStruct((map_side, depth, side), jnp.bfloat16)],
        scratch_shapes=[
            pltpu.VMEM(
                (height * depth // BLOCK**2, poses * WINDOW, BLOCK * BLOCK), jnp.bfloat16
            ),
        ],
        name="first_projection",
    )(*geo, density, pool_t)


def pick_kernel(owned, chips, bins_of, poses_of, classes_of, images, *refs):
    outs, order, filled = refs[:-2], refs[-2], refs[-1]
    groups = len(outs)
    each = outs[0].shape[0]
    side = images.shape[1]
    here, slab = lax.axis_index("bin"), lax.axis_index("slab")
    chip, core = slab // 2, lax.rem(slab, 2)
    lane = lax.broadcasted_iota(jnp.int32, (BLOCK, side), 1)

    def ahead(value, size):
        return jnp.where(value < 0, value + size, value)

    for slot in range(groups * each):
        order[slot] = -1
    for group in range(groups):
        filled[group] = 0
    for n in range(images.shape[0]):
        away = ahead(bins_of[n] - here, groups)
        rank = filled[away]
        filled[away] = rank + 1
        order[away * each + rank] = n
    for group in range(groups):
        for k in range(each):
            source = order[group * each + k]
            image = jnp.maximum(source, 0)
            outs[group][k, 0:side, :] = images[image]
            pose = poses_of[image]
            owner = pose // owned
            across = ahead(lax.rem(owner, 2) - core, 2)
            at = (across * chips + ahead(owner // 2 - chip, chips)) * owned + lax.rem(pose, owned)
            at = jnp.where(source >= 0, at, -1).astype(jnp.float32)
            named = classes_of[image].astype(jnp.float32)
            outs[group][k, side : side + BLOCK, :] = jnp.where(
                lane == 0, at, jnp.where(lane == 1, named, 0.0)
            ).astype(images.dtype)


def pick_images(images, image_bin, image_pose, image_class, owned, chips, groups):
    count, side, _ = images.shape
    each = count // 4
    out = jax.ShapeDtypeStruct((each, side + BLOCK, side), images.dtype)
    return pl.pallas_call(
        functools.partial(pick_kernel, owned, chips),
        in_specs=[smem()] * 3 + [vmem()],
        out_specs=[vmem()] * groups,
        out_shape=[out] * groups,
        scratch_shapes=[
            pltpu.SMEM((groups * each,), jnp.int32),
            pltpu.SMEM((groups,), jnp.int32),
        ],
        name="pick_images",
    )(image_bin, image_pose, image_class, images)


def times_hartley(value, table):
    _, side = value.shape
    high = value.astype(jnp.bfloat16)
    low = (value - high.astype(jnp.float32)).astype(jnp.bfloat16)
    both = jnp.dot(high, table, preferred_element_type=jnp.float32)
    rest = jnp.dot(low, table[:, :side], preferred_element_type=jnp.float32)
    return both[:, :side] + (both[:, side:] + rest)


def spectrum_kernel(groups, each, defocus, table, *refs):
    images, (keep, send, ctf, marks, label, sums, sem) = refs[:groups], refs[groups:]
    half = keep.shape[0]
    side = keep.shape[2]
    poses = 2 * half
    for group in range(groups):
        for k in range(each):
            at = group * each + k
            row = images[group][k, side : side + BLOCK, :].astype(jnp.float32)
            marks[at : at + 1, :] = row[0:1].astype(jnp.int32)
    copy = pltpu.make_async_copy(marks, label, sem)
    copy.start()
    sums[...] = jnp.zeros_like(sums)
    fill_ctf(ctf, defocus)
    hart = table[...]
    lane = lax.broadcasted_iota(jnp.int32, (8, side), 1)
    copy.wait()
    for group in range(groups):
        pixels = images[group][:, 0:side, :].reshape(each * side, side)
        both = jnp.dot(pixels, hart, preferred_element_type=jnp.float32)
        along = (both[:, :side] + both[:, side:]).reshape(each, side, side)
        turned = jnp.concatenate([along[k].T for k in range(each)], axis=0)
        full = times_hartley(turned, hart).reshape(each, side, side)
        for k in range(each):
            pose, kind = label[group * each + k, 0], label[group * each + k, 1]
            pose = jnp.where(pose < 0, poses, pose)
            sums[pose, 0:side, :] += ctf[kind] * full[k]
            sums[pose, side : side + 8, :] += jnp.where(lane == kind, 1.0, 0.0)
    for part, out in enumerate((keep, send)):
        for pose in range(half):
            out[pose, 0:side, :] = sums[part * half + pose, 0:side, :].T
            out[pose, side : side + 8, :] = sums[part * half + pose, side : side + 8, :]


def image_sums(images, defocus, table, poses):
    each, _, side = images[0].shape
    slots = each * len(images)
    half = jax.ShapeDtypeStruct((poses // 2, side + 8, side), jnp.float32)
    return pl.pallas_call(
        functools.partial(spectrum_kernel, len(images), each),
        in_specs=[smem(), vmem()] + [vmem()] * len(images),
        out_specs=[vmem()] * 3,
        out_shape=[half, half, jax.ShapeDtypeStruct((*defocus.shape, side, side), jnp.float32)],
        scratch_shapes=[
            pltpu.VMEM((slots, side), jnp.int32),
            pltpu.SMEM((slots, side), jnp.int32),
            pltpu.VMEM((poses + 1, side + 8, side), jnp.float32),
            pltpu.SemaphoreType.DMA(()),
        ],
        name="image_sums",
    )(defocus, table, *images)


def added(parts):
    return functools.reduce(jnp.add, [part[...].astype(jnp.float32) for part in parts])


def through(values, hart, change):
    owned, side, _ = values.shape

    def turn(rows):
        return jnp.concatenate([rows[k * side : (k + 1) * side].T for k in range(owned)], axis=0)

    full = times_hartley(turn(times_hartley(values.reshape(owned * side, side), hart)), hart)
    parts = [change(k, full[k * side : (k + 1) * side]) for k in range(owned)]
    field = times_hartley(turn(times_hartley(jnp.concatenate(parts, axis=0), hart)), hart)
    return field.reshape(owned, side, side)


def first_filter_kernel(weight, count, ctf, table, *refs):
    proj, totals, (field, residual, gains) = refs[:count], refs[count:-3], refs[-3:]
    _, side, _ = field.shape
    total = added(totals)

    def change(k, value):
        gain = jnp.zeros((side, side), jnp.float32)
        for c in range(ctf.shape[0]):
            gain = gain + total[k, side : side + 1, c : c + 1] * (ctf[c] * ctf[c])
        value = weight * (gain * value - total[k, 0:side, :])
        gains[k] = weight * gain
        residual[k] = value
        return value

    field[...] = through(added(proj), table[...], change).astype(field.dtype)


def first_field(proj, totals, ctf, table, weight, owned):
    side = table.shape[0]
    block = pl.BlockSpec((owned, side, side), lambda i: (0, 0, 0))
    tall = pl.BlockSpec((owned, side + 8, side), lambda i: (0, 0, 0))
    kept = jax.ShapeDtypeStruct((owned, side, side), jnp.float32)
    return pl.pallas_call(
        functools.partial(first_filter_kernel, weight, len(proj)),
        grid=(1,),
        in_specs=[vmem(), vmem()] + [block] * len(proj) + [tall] * len(totals),
        out_specs=[block] * 3,
        out_shape=[jax.ShapeDtypeStruct(kept.shape, jnp.bfloat16), kept, kept],
        name="first_field",
    )(ctf, table, *proj, *totals)


def next_filter_kernel(table, residual, gains, *refs):
    parts, field = refs[:-1], refs[-1]

    def change(k, value):
        return gains[k] * value + residual[k]

    field[...] = through(added(parts), table[...], change).astype(field.dtype)


def next_field(parts, residual, gains, table):
    block = pl.BlockSpec(residual.shape, lambda i: (0, 0, 0))
    return pl.pallas_call(
        next_filter_kernel,
        grid=(1,),
        in_specs=[vmem()] + [block] * (2 + len(parts)),
        out_specs=block,
        out_shape=jax.ShapeDtypeStruct(residual.shape, jnp.bfloat16),
        name="next_field",
    )(table, residual, gains, *parts)


def load_fields(field, fields):
    at = 0
    for part in fields:
        count = part.shape[0]
        field[at : at + count] = part[...].astype(jnp.float32)
        at += count


def gather_windows(f_ref, field, start, block, poses):
    for pose in range(poses):
        f_ref[pose * WINDOW : (pose + 1) * WINDOW, :] = field[
            pose, pl.ds(start[pose, block], WINDOW), :
        ].astype(jnp.bfloat16)


def step_gradient(split_ref, f_ref, field, turned, pool2, start, first_block, poses):
    height, depth, width = split_ref.shape
    for k in range(depth // BLOCK):
        planes = slice(k * BLOCK, (k + 1) * BLOCK)
        gather_windows(f_ref.at[k], field, start, first_block + k, poses)
        back = jnp.dot(turned[k], f_ref[k], preferred_element_type=jnp.float32)
        high = back.astype(jnp.bfloat16)
        low = (back - high.astype(jnp.float32)).astype(jnp.bfloat16)
        split_ref[:, planes, :] = jnp.concatenate([high, low], axis=1).reshape(
            height, BLOCK, width
        )
    return jnp.dot(
        split_ref[...].reshape(height * depth, width),
        pool2[...],
        preferred_element_type=jnp.float32,
    )


def step_kernel(
    map_side, poses, parts, bin_ref, start, sizes, dens, fold, windows, turned, pool2, pool_t, *refs
):
    fields = refs[:parts]
    first, keep, sent, field, f_ref, split_ref, send = refs[parts:]
    step = pl.program_id(0)

    @pl.when(step == 0)
    def _():
        keep[...] = jnp.zeros_like(keep)
        send[...] = jnp.zeros_like(send)
        load_fields(field, fields)

    height, depth, side = fold.shape
    count = depth // BLOCK
    grad = step_gradient(split_ref, f_ref, field, turned, pool2, start, step * count, poses)
    kept = dens[...].reshape(height * depth, map_side).astype(jnp.float32)
    moved = kept - sizes[0] * grad
    first[...] = moved.reshape(height, depth, map_side)
    folded = jnp.dot(moved.astype(jnp.bfloat16), pool_t[...], preferred_element_type=jnp.float32)
    before = fold[...].reshape(height * depth, side).astype(jnp.float32)
    change = folded.astype(jnp.bfloat16).astype(jnp.float32) - before
    high = change.astype(jnp.bfloat16)
    low = (change - high.astype(jnp.float32)).astype(jnp.bfloat16)
    split_ref[...] = jnp.concatenate([high, low], axis=1).reshape(height, depth, 2 * side)
    for k in range(count):
        pixels = split_ref[:, k * BLOCK : (k + 1) * BLOCK, :].reshape(BLOCK * BLOCK, 2 * side)
        prod = jnp.dot(windows[k], pixels, preferred_element_type=jnp.float32)
        prod = prod[:, :side] + prod[:, side:]
        add_projection((keep, send), prod, start, step * count + k, poses)

    @pl.when(step == pl.num_programs(0) - 1)
    def _():
        sent[...] = send[...].astype(sent.dtype)


def take_step(density, fold, fields, start, tables, sizes, bin_index, pool2, pool_t, row_share):
    map_side, depth, _ = density.shape
    side = pool_t.shape[1]
    poses = start.shape[0]
    half = jax.ShapeDtypeStruct((poses // 2, side, side), jnp.float32)
    row_blocks, count = row_share // BLOCK, depth // BLOCK

    def own(width):
        return pl.BlockSpec((BLOCK, depth, width), lambda i, at: (at[0] * row_blocks + i, 0, 0))

    return pl.pallas_call(
        functools.partial(step_kernel, map_side, poses, len(fields)),
        grid_spec=pltpu.PrefetchScalarGridSpec(
            num_scalar_prefetch=1,
            grid=(row_blocks,),
            in_specs=[smem()] * 2
            + [own(map_side), own(side)]
            + [pl.BlockSpec((count, *table.shape[1:]), lambda i, at: (i, 0, 0)) for table in tables]
            + [vmem()] * (2 + len(fields)),
            out_specs=[
                pl.BlockSpec((BLOCK, depth, map_side), lambda i, at: (i, 0, 0)), vmem(), vmem()
            ],
            scratch_shapes=[
                pltpu.VMEM((poses, side, side), jnp.float32),
                pltpu.VMEM((count, poses * WINDOW, side), jnp.bfloat16),
                pltpu.VMEM((BLOCK, depth, 2 * side), jnp.bfloat16),
                pltpu.VMEM(half.shape, jnp.float32),
            ],
        ),
        out_shape=[
            jax.ShapeDtypeStruct((row_share, depth, map_side), jnp.float32),
            half,
            jax.ShapeDtypeStruct(half.shape, jnp.bfloat16),
        ],
        name="take_step",
    )(bin_index.reshape(1), start, sizes, density, fold, *tables, pool2, pool_t, *fields)


def finish_kernel(poses, parts, start, sizes, first, turned, pool2, *refs):
    fields = refs[:parts]
    gradient, refined, field, f_ref, split_ref = refs[parts:]
    step = pl.program_id(0)

    @pl.when(step == 0)
    def _():
        load_fields(field, fields)

    count = first.shape[1] // BLOCK
    grad = step_gradient(split_ref, f_ref, field, turned, pool2, start, step * count, poses)
    grad = grad.reshape(first.shape)
    gradient[...] = grad
    refined[...] = first[...] - sizes[1] * grad


def finish(first, fields, start, turned, sizes, pool2):
    row_share, depth, map_side = first.shape
    side = pool2.shape[0] // 2
    poses = start.shape[0]
    count = depth // BLOCK
    rows = pl.BlockSpec((BLOCK, depth, map_side), lambda i: (i, 0, 0))
    out = jax.ShapeDtypeStruct(first.shape, jnp.float32)
    return pl.pallas_call(
        functools.partial(finish_kernel, poses, len(fields)),
        grid=(row_share // BLOCK,),
        in_specs=[smem()] * 2
        + [rows, pl.BlockSpec((count, *turned.shape[1:]), lambda i: (i, 0, 0))]
        + [vmem()] * (1 + len(fields)),
        out_specs=[rows, rows],
        out_shape=[out, out],
        scratch_shapes=[
            pltpu.VMEM((poses, side, side), jnp.float32),
            pltpu.VMEM((count, poses * WINDOW, side), jnp.bfloat16),
            pltpu.VMEM((BLOCK, depth, 2 * side), jnp.bfloat16),
        ],
        name="finish",
    )(start, sizes, first, turned, pool2, *fields)


def on_device(
    density, images, image_bin, image_pose, image_class, defocus, pose_offset, step_sizes
):
    bins = lax.axis_size("bin")
    slabs = lax.axis_size("slab")
    chips = slabs // 2
    bin_index = lax.axis_index("bin")
    map_side, depth, _ = density.shape
    image_count, side, _ = images.shape
    pose_count = pose_offset.shape[1]
    row_share = map_side // bins
    owned = pose_count // slabs
    weight = 16.0 * pose_count / (image_count * slabs)

    def to_core(value):
        return lax.ppermute(value, "slab", [(s, s ^ 1) for s in range(slabs)])

    def to_chip(value, shift):
        return lax.ppermute(
            value, "slab", [(s, (s + 2 * shift) % slabs) for s in range(slabs)]
        )

    def to_bin(value, shift):
        return lax.ppermute(value, "bin", [(b, (b + shift) % bins) for b in range(bins)])

    picked = pick_images(images, image_bin[:, 0], image_pose, image_class, owned, chips, bins)
    poses = bins * pose_count
    own_geo, geo, wide_geo = make_geometry(
        pose_offset, map_side, side, depth, row_share, chips, owned
    )
    pooling = pool_table(side, map_side).astype(jnp.bfloat16)
    pool_t = jnp.asarray(pooling.T)
    pool2 = jnp.asarray(np.concatenate([pooling, pooling], axis=0))
    table = hartley_table(side)

    picked, own_geo = lax.optimization_barrier((picked, own_geo))
    got_images = [picked[0]]
    for d in range(1, bins):
        got_images.append(to_bin(picked[d], d))

    def reduce_slab(keep, send, sent_as=jnp.float32):
        got = to_core(send)
        each = keep.shape[0] // chips

        def joined(d):
            rows = slice(d * each, (d + 1) * each)
            return (keep[rows] + got[rows].astype(jnp.float32)).astype(sent_as)

        return [keep, got] + [to_chip(joined(d), d) for d in range(1, chips)]

    keep, send, fold = first_projection(density, pool_t, own_geo, pose_count)
    keep, send, defocus = lax.optimization_barrier((keep, send, defocus))
    proj_parts = reduce_slab(keep, send)
    keep, send, ctf = image_sums(got_images, defocus, table, pose_count)
    total_parts = reduce_slab(keep, send)

    def share_field(field, early=(), late=()):
        near = [field] + [to_bin(field, bins - d) for d in range(1, bins)]
        near, early = lax.optimization_barrier((near, early))
        near = jnp.concatenate(near, axis=0)
        across = [to_chip(near, chips - d) for d in range(1, chips)]
        across, late = lax.optimization_barrier((across, late))
        row = [near] + across
        return row + [to_core(part) for part in row], early, late

    field, residual, gains = first_field(proj_parts, total_parts, ctf, table, weight, owned)
    field, geo, wide_geo = lax.optimization_barrier((field, geo, wide_geo))
    blocks = row_share // BLOCK * (depth // BLOCK)
    fields, turned, windows = share_field(
        field,
        turned_table(wide_geo, blocks, poses, map_side),
        window_table(geo, blocks, poses, map_side),
    )
    start = geo[2]
    first, keep, send = take_step(
        density, fold, fields, start, (windows, turned), step_sizes, bin_index, pool2, pool_t,
        row_share,
    )
    parts = reduce_slab(keep, send, jnp.bfloat16)

    def change(d):
        rows = slice(d * owned, (d + 1) * owned)
        return functools.reduce(jnp.add, [part[rows].astype(jnp.float32) for part in parts])

    moved = [to_bin(change(d).astype(jnp.bfloat16), d) for d in range(1, bins)]
    field = next_field(parts + moved, residual, gains, table)
    gradient, refined = finish(first, share_field(field)[0], start, turned, step_sizes, pool2)
    return (gradient, refined)


def solution(mesh):
    return jax.shard_map(
        on_device,
        mesh=mesh,
        in_specs=(
            P("grp", "slab", None),
            P(("grp", "bin", "slab"), None, None),
            P(("grp", "bin", "slab"), None),
            P(("grp", "bin", "slab")),
            P(("grp", "bin", "slab")),
            P("grp"),
            P("grp", None),
            P(),
        ),
        out_specs=(P(("grp", "bin"), "slab", None), P(("grp", "bin"), "slab", None)),
        check_vma=False,
    )
```

profile of v0, /device:TPU:0, one launch (start us, length us, event | category | flops | bytes accessed | tf_op | source)
XLA Modules:
  0.0 124.6 jit_solution(11270183233686930195)
XLA Ops:
  0.6 1.6 %geometry.1 = (f32[8,128]{1,0:T(8,128)}, f32[8,128]{1,0:T(8,128)}, s32[8,128]{1,0:T(8,128)}, f32[8,128]{1,0:T(8,128)}, f32[32,128]{1,0:T(8,128)}, /*index=5*/f32...) custom-call(f32[4,8]{1,0:T(4,128)} %offsets.1), custom_call_target="tpu_custom_call" | custom-call | tf_op jit(solution)/shard_map/geometry/pallas_call | solution.py:177
  2.2 2.2 %pick_images.1 = (bf16[4,144,128]{2,1,0:T(8,128)(2,1)}, bf16[4,144,128]{2,1,0:T(8,128)(2,1)}, bf16[4,144,128]{2,1,0:T(8,128)(2,1)}, bf16[4,144,128]{2,1,0:T(8,128)(2,1)}) custom-call(s32[16]{0:T(128)} %bitcast.2, s32[16]{0:T(128)} %poses_of.1, s32[16]{0:T(128)} %classes_of.1, bf16[16,128,128]{2,1,0:T(8,128)(2,1)} %images.1), custom_call_target="tpu_custom_call" | custom-call | tf_op jit(solution)/shard_map/pick_images/pallas_call | solution.py:360
  4.4 3.1 %collective-permute-start = (bf16[4,144,128]{2,1,0:T(8,128)(2,1)}, bf16[4,144,128]{2,1,0:T(8,128)(2,1)S(1)}, u32[]{:S(2)}, u32[]{:S(2)}) collective-permute-start(bf16[4,144,128]{2,1,0:T(8,128)(2,1)} %get-tuple-element.73), channel_id=1, source_target_pairs={{0,4},{4,8},{8,12},{12,0},{1,5},{5,9},{9,13},{13,1},{2,6},{6,10},{... | collective-permute-start | bytes 442376 | tf_op jit(solution)/shard_map/ppermute | solution.py:674
  7.4 2.6 %collective-permute-start.1 = (bf16[4,144,128]{2,1,0:T(8,128)(2,1)}, bf16[4,144,128]{2,1,0:T(8,128)(2,1)S(1)}, u32[]{:S(2)}, u32[]{:S(2)}) collective-permute-start(bf16[4,144,128]{2,1,0:T(8,128)(2,1)} %get-tuple-element.74), channel_id=1, source_target_pairs={{0,8},{4,12},{8,0},{12,4},{1,9},{5,13},{9,1},{13,5},{2,10},{6,14},... | collective-permute-start | bytes 442376 | tf_op jit(solution)/shard_map/ppermute | solution.py:674
  10.0 1.3 %collective-permute-start.2 = (bf16[4,144,128]{2,1,0:T(8,128)(2,1)}, bf16[4,144,128]{2,1,0:T(8,128)(2,1)S(1)}, u32[]{:S(2)}, u32[]{:S(2)}) collective-permute-start(bf16[4,144,128]{2,1,0:T(8,128)(2,1)} %get-tuple-element.75), channel_id=1, source_target_pairs={{0,12},{4,0},{8,4},{12,8},{1,13},{5,1},{9,5},{13,9},{2,14},{6,2},{... | collective-permute-start | bytes 442376 | tf_op jit(solution)/shard_map/ppermute | solution.py:674
  11.4 10.6 %first_projection.1 = (f32[4,128,128]{2,1,0:T(8,128)}, f32[4,128,128]{2,1,0:T(8,128)}, bf16[256,64,128]{2,1,0:T(8,128)(2,1)}) custom-call(f32[8,128]{1,0:T(8,128)} %get-tuple-element.65.cosine, f32[8,128]{1,0:T(8,128)} %get-tuple-element.66.sine, s32[8,128]{1,0:T(8,128)} %get-tuple-element.67.start, f32[8,128]{1,0:T(8,128)} %get-tuple-element.68.offset, ...), custom_call_target="tpu_custom_call" | custom-call | tf_op jit(solution)/shard_map/first_projection/pallas_call | solution.py:302
  22.0 0.0 collective-permute-done.refs_1_
  22.0 0.0 collective-permute-done.2.refs_3_
  22.1 0.6 copy-done.12
  22.7 0.1 copy-done.13
  22.8 0.6 copy-done.14
  23.4 5.4 %image_sums.1 = (f32[4,136,128]{2,1,0:T(8,128)}, f32[4,136,128]{2,1,0:T(8,128)}, f32[16,128,128]{2,1,0:T(8,128)}) custom-call(f32[16]{0:T(128)} %defocus, bf16[128,256]{1,0:T(8,128)(2,1)} %constant.13.clone.table, bf16[4,144,128]{2,1,0:T(8,128)(2,1)} %get-tuple-element.72.refs_0_, bf16[4,144,128]{2,1,0:T(8,128)(2,1)} %copy-done.12, ...), custom_call_target="tpu_custom_call" | custom-call | tf_op jit(solution)/shard_map/image_sums/pallas_call | solution.py:420
  28.8 0.1 collective-permute-start.5
  28.9 0.5 collective-permute-start.3
  29.4 1.3 %collective-permute-done.5.refs_4_ = f32[4,136,128]{2,1,0:T(8,128)S(1)} collective-permute-done((f32[4,136,128]{2,1,0:T(8,128)}, f32[4,136,128]{2,1,0:T(8,128)S(1)}, u32[]{:S(2)}, u32[]{:S(2)}) %collective-permute-start.5) | collective-permute-done | bytes 278560 | tf_op jit(solution)/shard_map/ppermute | solution.py:666
  30.6 1.0 slice_add_fusion
  31.7 1.6 %collective-permute-start.6 = (f32[2,136,128]{2,1,0:T(8,128)S(1)}, f32[2,136,128]{2,1,0:T(8,128)S(1)}, u32[]{:S(2)}, u32[]{:S(2)}) collective-permute-start(f32[2,136,128]{2,1,0:T(8,128)S(1)} %slice_add_fusion), channel_id=1, source_target_pairs={{0,2},{1,3},{2,0},{3,1},{4,6},{5,7},{6,4},{7,5},{8,10},{9,11},{10,... | collective-permute-start | bytes 417800 | tf_op jit(solution)/shard_map/ppermute | solution.py:669
  33.2 0.0 collective-permute-done.3.refs_1_
  33.2 1.0 slice_add_fusion.1
  34.3 0.6 collective-permute-start.4
  34.8 5.4 %collective-permute-done.4.refs_2_ = f32[2,128,128]{2,1,0:T(8,128)S(1)} collective-permute-done((f32[2,128,128]{2,1,0:T(8,128)S(1)}, f32[2,128,128]{2,1,0:T(8,128)S(1)}, u32[]{:S(2)}, u32[]{:S(2)}) %collective-permute-start.4) | collective-permute-done | bytes 131104 | tf_op jit(solution)/shard_map/ppermute | solution.py:669
  40.3 0.6 copy-done.16
  40.9 0.0 copy-done.15
  41.0 3.0 %first_field.1 = (bf16[2,128,128]{2,1,0:T(8,128)(2,1)}, f32[2,128,128]{2,1,0:T(8,128)}, f32[2,128,128]{2,1,0:T(8,128)}) custom-call(f32[16,128,128]{2,1,0:T(8,128)} %get-tuple-element.76.ctf, bf16[128,256]{1,0:T(8,128)(2,1)} %constant.13.clone.table, f32[4,128,128]{2,1,0:T(8,128)} %get-tuple-element.77.refs_0_, f32[4,128,128]{2,1,0:T(8,128)} %copy-done.3, ...), custom_call_target="tpu_custom_call" | custom-call | tf_op jit(solution)/shard_map/first_field/pallas_call | solution.py:473
  44.0 0.8 collective-permute-start.9
  44.8 2.3 %collective-permute-start.8 = (bf16[2,128,128]{2,1,0:T(8,128)(2,1)}, bf16[2,128,128]{2,1,0:T(8,128)(2,1)S(1)}, u32[]{:S(2)}, u32[]{:S(2)}) collective-permute-start(bf16[2,128,128]{2,1,0:T(8,128)(2,1)} %get-tuple-element.93), channel_id=1, source_target_pairs={{0,8},{4,12},{8,0},{12,4},{1,9},{5,13},{9,1},{13,5},{2,10},{6,14},... | collective-permute-start | bytes 196616 | tf_op jit(solution)/shard_map/ppermute | solution.py:674
  47.1 0.8 collective-permute-start.7
  47.8 4.1 %shard_map.122.turned = bf16[16,256,512]{2,1,0:T(8,128)(2,1)} custom-call(f32[2,512]{1,0:T(2,128)} %get-tuple-element.91.wide, f32[16,512]{1,0:T(8,128)} %get-tuple-element.92.lanes), custom_call_target="tpu_custom_call" | custom-call | tf_op jit(solution)/shard_map/pallas_call | solution.py:234
  51.9 0.0 collective-permute-done.9
  51.9 0.5 collective-permute-done.8
  52.4 1.5 %collective-permute-start.10 = (bf16[8,128,128]{2,1,0:T(8,128)(2,1)S(1)}, bf16[8,128,128]{2,1,0:T(8,128)(2,1)S(1)}, u32[]{:S(2)}, u32[]{:S(2)}) collective-permute-start(bf16[8,128,128]{2,1,0:T(8,128)(2,1)S(1)} %constant_dynamic-update-slice_fusion.refs_0_), channel_id=1, source_target_pairs={{0,2},{1,3},{2,0},{3,1},{4,6},{5,7},{6,4},{7,5},{8,10},{9,11},{10,... | collective-permute-start | bytes 786440 | tf_op jit(solution)/shard_map/ppermute | solution.py:669
  53.9 5.2 %shard_map.123.windows = bf16[16,512,256]{2,1,0:T(8,128)(2,1)} custom-call(f32[32,128]{1,0:T(8,128)} %get-tuple-element.97.cosine, f32[32,128]{1,0:T(8,128)} %get-tuple-element.98.sine, s32[32,128]{1,0:T(8,128)} %get-tuple-element.88.start, f32[32,128]{1,0:T(8,128)} %get-tuple-element.99.offset), custom_call_target="tpu_custom_call" | custom-call | tf_op jit(solution)/shard_map/pallas_call | solution.py:234
  59.1 0.0 collective-permute-start.11
  59.1 0.1 collective-permute-done.10.refs_1_
  59.2 0.5 collective-permute-start.12
  59.6 1.0 collective-permute-done.11.refs_2_
  60.6 0.4 collective-permute-done.12.refs_3_
  61.0 0.3 copy-done.7
  61.3 0.4 copy-done.8
  61.7 10.7 %take_step.1 = (f32[64,64,256]{2,1,0:T(8,128)}, f32[16,128,128]{2,1,0:T(8,128)}, bf16[16,128,128]{2,1,0:T(8,128)(2,1)}) custom-call(s32[1]{0:T(128)} %bitcast.1.bin_ref, s32[32,128]{1,0:T(8,128)} %get-tuple-element.88.start, f32[2]{0:T(128)} %sizes.3, bf16[256,64,256]{2,1,0:T(8,128)(2,1)} %dens.3, bf16[256,64,128]{2,1,0:T(8,128)(2,1)} %get-tuple-element.89.fold, ...), custom_call_target="tpu_custom_call" | custom-call | tf_op jit(solution)/shard_map/take_step/pallas_call | solution.py:583
  72.4 0.2 collective-permute-start.13
  72.7 2.0 %collective-permute-done.13.refs_1_ = bf16[16,128,128]{2,1,0:T(8,128)(2,1)S(1)} collective-permute-done((bf16[16,128,128]{2,1,0:T(8,128)(2,1)}, bf16[16,128,128]{2,1,0:T(8,128)(2,1)S(1)}, u32[]{:S(2)}, u32[]{:S(2)}) %collective-permute-start.13) | collective-permute-done | bytes 524320 | tf_op jit(solution)/shard_map/ppermute | solution.py:666
  74.6 1.3 %add_convert_fusion = bf16[8,128,128]{2,1,0:T(8,128)(2,1)S(1)} fusion(f32[16,128,128]{2,1,0:T(8,128)} %get-tuple-element.106.refs_0_, bf16[16,128,128]{2,1,0:T(8,128)(2,1)S(1)} %collective-permute-done.13.refs_1_), kind=kLoop, calls=%fused_computation | loop fusion | flops 393216 | bytes 1048576 | tf_op jit(solution)/shard_map/convert_element_type | solution.py:697
  75.9 1.1 collective-permute-start.14
  77.0 7.3 %collective-permute-done.14.refs_2_ = bf16[8,128,128]{2,1,0:T(8,128)(2,1)S(1)} collective-permute-done((bf16[8,128,128]{2,1,0:T(8,128)(2,1)S(1)}, bf16[8,128,128]{2,1,0:T(8,128)(2,1)S(1)}, u32[]{:S(2)}, u32[]{:S(2)}) %collective-permute-start.14) | collective-permute-done | bytes 262176 | tf_op jit(solution)/shard_map/ppermute | solution.py:669
  84.4 1.2 add_convert_fusion.1
  85.6 3.5 %collective-permute-start.17 = (bf16[2,128,128]{2,1,0:T(8,128)(2,1)S(1)}, bf16[2,128,128]{2,1,0:T(8,128)(2,1)S(1)}, u32[]{:S(2)}, u32[]{:S(2)}) collective-permute-start(bf16[2,128,128]{2,1,0:T(8,128)(2,1)S(1)} %get-tuple-element.112), channel_id=1, source_target_pairs={{0,12},{4,0},{8,4},{12,8},{1,13},{5,1},{9,5},{13,9},{2,14},{6,2},{... | collective-permute-start | bytes 196616 | tf_op jit(solution)/shard_map/ppermute | solution.py:674
  89.0 0.3 collective-permute-start.16
  89.4 0.3 collective-permute-start.15
  89.7 1.6 %collective-permute-done.17.refs_5_ = bf16[2,128,128]{2,1,0:T(8,128)(2,1)S(1)} collective-permute-done((bf16[2,128,128]{2,1,0:T(8,128)(2,1)S(1)}, bf16[2,128,128]{2,1,0:T(8,128)(2,1)S(1)}, u32[]{:S(2)}, u32[]{:S(2)}) %collective-permute-start.17) | collective-permute-done | bytes 65568 | tf_op jit(solution)/shard_map/ppermute | solution.py:674
  91.3 3.3 %collective-permute-done.16.refs_4_ = bf16[2,128,128]{2,1,0:T(8,128)(2,1)S(1)} collective-permute-done((bf16[2,128,128]{2,1,0:T(8,128)(2,1)S(1)}, bf16[2,128,128]{2,1,0:T(8,128)(2,1)S(1)}, u32[]{:S(2)}, u32[]{:S(2)}) %collective-permute-start.16) | collective-permute-done | bytes 65568 | tf_op jit(solution)/shard_map/ppermute | solution.py:674
  94.6 0.9 collective-permute-done.15.refs_3_
  95.5 0.6 copy-done.19
  96.1 2.5 %next_field.1 = bf16[2,128,128]{2,1,0:T(8,128)(2,1)} custom-call(bf16[128,256]{1,0:T(8,128)(2,1)} %constant.13.clone.table, f32[2,128,128]{2,1,0:T(8,128)} %get-tuple-element.104.residual, f32[2,128,128]{2,1,0:T(8,128)} %get-tuple-element.105.gains, f32[16,128,128]{2,1,0:T(8,128)} %get-tuple-element.106.refs_0_, bf16[16,128,128]{2,1,0:T(8,128)(2,1)} %copy-done, ...), custom_call_target="tpu_custom_call" | custom-call | tf_op jit(solution)/shard_map/next_field/pallas_call | solution.py:494
  98.6 2.0 %collective-permute-start.19 = (bf16[2,128,128]{2,1,0:T(8,128)(2,1)}, bf16[2,128,128]{2,1,0:T(8,128)(2,1)S(1)}, u32[]{:S(2)}, u32[]{:S(2)}) collective-permute-start(bf16[2,128,128]{2,1,0:T(8,128)(2,1)} %next_field.1), channel_id=1, source_target_pairs={{0,8},{4,12},{8,0},{12,4},{1,9},{5,13},{9,1},{13,5},{2,10},{6,14},... | collective-permute-start | bytes 196616 | tf_op jit(solution)/shard_map/ppermute | solution.py:674
  100.6 2.2 %collective-permute-start.18 = (bf16[2,128,128]{2,1,0:T(8,128)(2,1)}, bf16[2,128,128]{2,1,0:T(8,128)(2,1)S(1)}, u32[]{:S(2)}, u32[]{:S(2)}) collective-permute-start(bf16[2,128,128]{2,1,0:T(8,128)(2,1)} %next_field.1), channel_id=1, source_target_pairs={{0,12},{4,0},{8,4},{12,8},{1,13},{5,1},{9,5},{13,9},{2,14},{6,2},{... | collective-permute-start | bytes 196616 | tf_op jit(solution)/shard_map/ppermute | solution.py:674
  102.8 2.3 %collective-permute-done.20 = bf16[2,128,128]{2,1,0:T(8,128)(2,1)S(1)} collective-permute-done((bf16[2,128,128]{2,1,0:T(8,128)(2,1)}, bf16[2,128,128]{2,1,0:T(8,128)(2,1)S(1)}, u32[]{:S(2)}, u32[]{:S(2)}) %collective-permute-start.20) | collective-permute-done | bytes 65568 | tf_op jit(solution)/shard_map/ppermute | solution.py:674
  105.1 1.2 collective-permute-done.19
  106.3 0.8 constant_dynamic-update-slice_fusion.7
  107.2 1.4 %collective-permute-start.21 = (bf16[8,128,128]{2,1,0:T(8,128)(2,1)S(1)}, bf16[8,128,128]{2,1,0:T(8,128)(2,1)S(1)}, u32[]{:S(2)}, u32[]{:S(2)}) collective-permute-start(bf16[8,128,128]{2,1,0:T(8,128)(2,1)S(1)} %constant_dynamic-update-slice_fusion.4.refs_0_), channel_id=1, source_target_pairs={{0,2},{1,3},{2,0},{3,1},{4,6},{5,7},{6,4},{7,5},{8,10},{9,11},{10,... | collective-permute-start | bytes 786440 | tf_op jit(solution)/shard_map/ppermute | solution.py:669
  108.6 5.1 %collective-permute-done.21.refs_1_ = bf16[8,128,128]{2,1,0:T(8,128)(2,1)S(1)} collective-permute-done((bf16[8,128,128]{2,1,0:T(8,128)(2,1)S(1)}, bf16[8,128,128]{2,1,0:T(8,128)(2,1)S(1)}, u32[]{:S(2)}, u32[]{:S(2)}) %collective-permute-start.21) | collective-permute-done | bytes 262176 | tf_op jit(solution)/shard_map/ppermute | solution.py:669
  113.7 1.5 %collective-permute-done.23.refs_3_ = bf16[8,128,128]{2,1,0:T(8,128)(2,1)S(1)} collective-permute-done((bf16[8,128,128]{2,1,0:T(8,128)(2,1)S(1)}, bf16[8,128,128]{2,1,0:T(8,128)(2,1)S(1)}, u32[]{:S(2)}, u32[]{:S(2)}) %collective-permute-start.23) | collective-permute-done | bytes 262176 | tf_op jit(solution)/shard_map/ppermute | solution.py:666
  115.2 0.7 copy-done.11
  115.9 8.6 %finish.1 = (f32[64,64,256]{2,1,0:T(8,128)}, f32[64,64,256]{2,1,0:T(8,128)}) custom-call(s32[32,128]{1,0:T(8,128)} %get-tuple-element.88.start, f32[2]{0:T(128)} %sizes.3, f32[64,64,256]{2,1,0:T(8,128)} %get-tuple-element.103.first, bf16[16,256,512]{2,1,0:T(8,128)(2,1)} %shard_map.122.turned, bf16[256,256]{1,0:T(8,128)(2,1)} %constant.12.clone.pool2, ...), custom_call_target="tpu_custom_call" | custom-call | tf_op jit(solution)/shard_map/finish/pallas_call | solution.py:634
  (48 shorter events, 0.2 us)
Async XLA Ops:
  4.4 17.6 %collective-permute-start = (bf16[4,144,128]{2,1,0:T(8,128)(2,1)}, bf16[4,144,128]{2,1,0:T(8,128)(2,1)S(1)}, u32[]{:S(2)}, u32[]{:S(2)}) collective-permute-start(bf16[4,144,128]{2,1,0:T(8,128)(2,1)} %get-tuple-element.73), channel_id=1, source_target_pairs={{0,4},{4,8},{8,12},{12,0},{1,5},{5,9},{9,13},{13,1},{2,6},{6,10},{... | collective-permute-start | bytes 442376 | tf_op jit(solution)/shard_map/ppermute | solution.py:674
  7.4 14.6 %collective-permute-start.1 = (bf16[4,144,128]{2,1,0:T(8,128)(2,1)}, bf16[4,144,128]{2,1,0:T(8,128)(2,1)S(1)}, u32[]{:S(2)}, u32[]{:S(2)}) collective-permute-start(bf16[4,144,128]{2,1,0:T(8,128)(2,1)} %get-tuple-element.74), channel_id=1, source_target_pairs={{0,8},{4,12},{8,0},{12,4},{1,9},{5,13},{9,1},{13,5},{2,10},{6,14},... | collective-permute-start | bytes 442376 | tf_op jit(solution)/shard_map/ppermute | solution.py:674
  10.0 12.0 %collective-permute-start.2 = (bf16[4,144,128]{2,1,0:T(8,128)(2,1)}, bf16[4,144,128]{2,1,0:T(8,128)(2,1)S(1)}, u32[]{:S(2)}, u32[]{:S(2)}) collective-permute-start(bf16[4,144,128]{2,1,0:T(8,128)(2,1)} %get-tuple-element.75), channel_id=1, source_target_pairs={{0,12},{4,0},{8,4},{12,8},{1,13},{5,1},{9,5},{13,9},{2,14},{6,2},{... | collective-permute-start | bytes 442376 | tf_op jit(solution)/shard_map/ppermute | solution.py:674
  22.0 0.7 copy-start.12
  22.0 0.7 copy-start.13
  22.8 0.7 copy-start.14
  28.8 1.8 %collective-permute-start.5 = (f32[4,136,128]{2,1,0:T(8,128)}, f32[4,136,128]{2,1,0:T(8,128)S(1)}, u32[]{:S(2)}, u32[]{:S(2)}) collective-permute-start(f32[4,136,128]{2,1,0:T(8,128)} %get-tuple-element.80), channel_id=1, source_target_pairs={{0,1},{1,0},{2,3},{3,2},{4,5},{5,4},{6,7},{7,6},{8,9},{9,8},{10,11... | collective-permute-start | bytes 835592 | tf_op jit(solution)/shard_map/ppermute | solution.py:666
  28.9 4.4 %collective-permute-start.3 = (f32[4,128,128]{2,1,0:T(8,128)}, f32[4,128,128]{2,1,0:T(8,128)S(1)}, u32[]{:S(2)}, u32[]{:S(2)}) collective-permute-start(f32[4,128,128]{2,1,0:T(8,128)} %get-tuple-element.78), channel_id=1, source_target_pairs={{0,1},{1,0},{2,3},{3,2},{4,5},{5,4},{6,7},{7,6},{8,9},{9,8},{10,11... | collective-permute-start | bytes 786440 | tf_op jit(solution)/shard_map/ppermute | solution.py:666
  30.6 9.6 %copy-start.2 = (f32[4,136,128]{2,1,0:T(8,128)}, f32[4,136,128]{2,1,0:T(8,128)S(1)}, u32[]{:S(2)}) copy-start(f32[4,136,128]{2,1,0:T(8,128)S(1)} %collective-permute-done.5.refs_4_) | copy-start | bytes 835588
  31.7 8.6 %collective-permute-start.6 = (f32[2,136,128]{2,1,0:T(8,128)S(1)}, f32[2,136,128]{2,1,0:T(8,128)S(1)}, u32[]{:S(2)}, u32[]{:S(2)}) collective-permute-start(f32[2,136,128]{2,1,0:T(8,128)S(1)} %slice_add_fusion), channel_id=1, source_target_pairs={{0,2},{1,3},{2,0},{3,1},{4,6},{5,7},{6,4},{7,5},{8,10},{9,11},{10,... | collective-permute-start | bytes 417800 | tf_op jit(solution)/shard_map/ppermute | solution.py:669
  33.2 7.0 %copy-start.3 = (f32[4,128,128]{2,1,0:T(8,128)}, f32[4,128,128]{2,1,0:T(8,128)S(1)}, u32[]{:S(2)}) copy-start(f32[4,128,128]{2,1,0:T(8,128)S(1)} %collective-permute-done.3.refs_1_) | copy-start | bytes 786436
  34.3 6.0 %collective-permute-start.4 = (f32[2,128,128]{2,1,0:T(8,128)S(1)}, f32[2,128,128]{2,1,0:T(8,128)S(1)}, u32[]{:S(2)}, u32[]{:S(2)}) collective-permute-start(f32[2,128,128]{2,1,0:T(8,128)S(1)} %slice_add_fusion.1), channel_id=1, source_target_pairs={{0,2},{1,3},{2,0},{3,1},{4,6},{5,7},{6,4},{7,5},{8,10},{9,11},{10,... | collective-permute-start | bytes 393224 | tf_op jit(solution)/shard_map/ppermute | solution.py:669
  40.3 0.7 copy-start.16
  40.3 0.7 copy-start.15
  44.0 8.4 %copy-start.20 = (bf16[2,128,128]{2,1,0:T(8,128)(2,1)S(1)}, bf16[2,128,128]{2,1,0:T(8,128)(2,1)}, u32[]{:S(2)}) copy-start(bf16[2,128,128]{2,1,0:T(8,128)(2,1)} %get-tuple-element.93) | copy-start | bytes 196612
  44.0 7.9 %collective-permute-start.9 = (bf16[2,128,128]{2,1,0:T(8,128)(2,1)}, bf16[2,128,128]{2,1,0:T(8,128)(2,1)S(1)}, u32[]{:S(2)}, u32[]{:S(2)}) collective-permute-start(bf16[2,128,128]{2,1,0:T(8,128)(2,1)} %get-tuple-element.93), channel_id=1, source_target_pairs={{0,4},{4,8},{8,12},{12,0},{1,5},{5,9},{9,13},{13,1},{2,6},{6,10},{... | collective-permute-start | bytes 196616 | tf_op jit(solution)/shard_map/ppermute | solution.py:674
  44.8 7.6 %collective-permute-start.8 = (bf16[2,128,128]{2,1,0:T(8,128)(2,1)}, bf16[2,128,128]{2,1,0:T(8,128)(2,1)S(1)}, u32[]{:S(2)}, u32[]{:S(2)}) collective-permute-start(bf16[2,128,128]{2,1,0:T(8,128)(2,1)} %get-tuple-element.93), channel_id=1, source_target_pairs={{0,8},{4,12},{8,0},{12,4},{1,9},{5,13},{9,1},{13,5},{2,10},{6,14},... | collective-permute-start | bytes 196616 | tf_op jit(solution)/shard_map/ppermute | solution.py:674
  47.1 5.3 %collective-permute-start.7 = (bf16[2,128,128]{2,1,0:T(8,128)(2,1)}, bf16[2,128,128]{2,1,0:T(8,128)(2,1)S(1)}, u32[]{:S(2)}, u32[]{:S(2)}) collective-permute-start(bf16[2,128,128]{2,1,0:T(8,128)(2,1)} %get-tuple-element.93), channel_id=1, source_target_pairs={{0,12},{4,0},{8,4},{12,8},{1,13},{5,1},{9,5},{13,9},{2,14},{6,2},{... | collective-permute-start | bytes 196616 | tf_op jit(solution)/shard_map/ppermute | solution.py:674
  52.4 8.6 %copy-start.4 = (bf16[8,128,128]{2,1,0:T(8,128)(2,1)}, bf16[8,128,128]{2,1,0:T(8,128)(2,1)S(1)}, u32[]{:S(2)}) copy-start(bf16[8,128,128]{2,1,0:T(8,128)(2,1)S(1)} %constant_dynamic-update-slice_fusion.refs_0_) | copy-start | bytes 786436
  52.4 6.7 %collective-permute-start.10 = (bf16[8,128,128]{2,1,0:T(8,128)(2,1)S(1)}, bf16[8,128,128]{2,1,0:T(8,128)(2,1)S(1)}, u32[]{:S(2)}, u32[]{:S(2)}) collective-permute-start(bf16[8,128,128]{2,1,0:T(8,128)(2,1)S(1)} %constant_dynamic-update-slice_fusion.refs_0_), channel_id=1, source_target_pairs={{0,2},{1,3},{2,0},{3,1},{4,6},{5,7},{6,4},{7,5},{8,10},{9,11},{10,... | collective-permute-start | bytes 786440 | tf_op jit(solution)/shard_map/ppermute | solution.py:669
  59.1 1.5 %collective-permute-start.11 = (bf16[8,128,128]{2,1,0:T(8,128)(2,1)S(1)}, bf16[8,128,128]{2,1,0:T(8,128)(2,1)S(1)}, u32[]{:S(2)}, u32[]{:S(2)}) collective-permute-start(bf16[8,128,128]{2,1,0:T(8,128)(2,1)S(1)} %constant_dynamic-update-slice_fusion.refs_0_), channel_id=1, source_target_pairs={{0,1},{1,0},{2,3},{3,2},{4,5},{5,4},{6,7},{7,6},{8,9},{9,8},{10,11... | collective-permute-start | bytes 786440 | tf_op jit(solution)/shard_map/ppermute | solution.py:666
  59.2 1.9 %copy-start.6 = (bf16[8,128,128]{2,1,0:T(8,128)(2,1)}, bf16[8,128,128]{2,1,0:T(8,128)(2,1)S(1)}, u32[]{:S(2)}) copy-start(bf16[8,128,128]{2,1,0:T(8,128)(2,1)S(1)} %collective-permute-done.10.refs_1_) | copy-start | bytes 786436
  59.2 1.8 %collective-permute-start.12 = (bf16[8,128,128]{2,1,0:T(8,128)(2,1)S(1)}, bf16[8,128,128]{2,1,0:T(8,128)(2,1)S(1)}, u32[]{:S(2)}, u32[]{:S(2)}) collective-permute-start(bf16[8,128,128]{2,1,0:T(8,128)(2,1)S(1)} %collective-permute-done.10.refs_1_), channel_id=1, source_target_pairs={{0,1},{1,0},{2,3},{3,2},{4,5},{5,4},{6,7},{7,6},{8,9},{9,8},{10,11... | collective-permute-start | bytes 786440 | tf_op jit(solution)/shard_map/ppermute | solution.py:666
  60.6 0.7 copy-start.7
  61.0 0.7 copy-start.8
  72.4 2.2 %collective-permute-start.13 = (bf16[16,128,128]{2,1,0:T(8,128)(2,1)}, bf16[16,128,128]{2,1,0:T(8,128)(2,1)S(1)}, u32[]{:S(2)}, u32[]{:S(2)}) collective-permute-start(bf16[16,128,128]{2,1,0:T(8,128)(2,1)} %get-tuple-element.107), channel_id=1, source_target_pairs={{0,1},{1,0},{2,3},{3,2},{4,5},{5,4},{6,7},{7,6},{8,9},{9,8},{10,11... | collective-permute-start | bytes 1572872 | tf_op jit(solution)/shard_map/ppermute | solution.py:666
  74.6 20.8 %copy-start = (bf16[16,128,128]{2,1,0:T(8,128)(2,1)}, bf16[16,128,128]{2,1,0:T(8,128)(2,1)S(1)}, u32[]{:S(2)}) copy-start(bf16[16,128,128]{2,1,0:T(8,128)(2,1)S(1)} %collective-permute-done.13.refs_1_) | copy-start | bytes 1572868
  75.9 8.4 %collective-permute-start.14 = (bf16[8,128,128]{2,1,0:T(8,128)(2,1)S(1)}, bf16[8,128,128]{2,1,0:T(8,128)(2,1)S(1)}, u32[]{:S(2)}, u32[]{:S(2)}) collective-permute-start(bf16[8,128,128]{2,1,0:T(8,128)(2,1)S(1)} %add_convert_fusion), channel_id=1, source_target_pairs={{0,2},{1,3},{2,0},{3,1},{4,6},{5,7},{6,4},{7,5},{8,10},{9,11},{10,... | collective-permute-start | bytes 786440 | tf_op jit(solution)/shard_map/ppermute | solution.py:669
  84.4 11.1 %copy-start.1 = (bf16[8,128,128]{2,1,0:T(8,128)(2,1)}, bf16[8,128,128]{2,1,0:T(8,128)(2,1)S(1)}, u32[]{:S(2)}) copy-start(bf16[8,128,128]{2,1,0:T(8,128)(2,1)S(1)} %collective-permute-done.14.refs_2_) | copy-start | bytes 786436
  85.6 5.7 %collective-permute-start.17 = (bf16[2,128,128]{2,1,0:T(8,128)(2,1)S(1)}, bf16[2,128,128]{2,1,0:T(8,128)(2,1)S(1)}, u32[]{:S(2)}, u32[]{:S(2)}) collective-permute-start(bf16[2,128,128]{2,1,0:T(8,128)(2,1)S(1)} %get-tuple-element.112), channel_id=1, source_target_pairs={{0,12},{4,0},{8,4},{12,8},{1,13},{5,1},{9,5},{13,9},{2,14},{6,2},{... | collective-permute-start | bytes 196616 | tf_op jit(solution)/shard_map/ppermute | solution.py:674
  89.0 5.5 %collective-permute-start.16 = (bf16[2,128,128]{2,1,0:T(8,128)(2,1)S(1)}, bf16[2,128,128]{2,1,0:T(8,128)(2,1)S(1)}, u32[]{:S(2)}, u32[]{:S(2)}) collective-permute-start(bf16[2,128,128]{2,1,0:T(8,128)(2,1)S(1)} %get-tuple-element.113), channel_id=1, source_target_pairs={{0,8},{4,12},{8,0},{12,4},{1,9},{5,13},{9,1},{13,5},{2,10},{6,14},... | collective-permute-start | bytes 196616 | tf_op jit(solution)/shard_map/ppermute | solution.py:674
  89.4 6.1 %collective-permute-start.15 = (bf16[2,128,128]{2,1,0:T(8,128)(2,1)S(1)}, bf16[2,128,128]{2,1,0:T(8,128)(2,1)S(1)}, u32[]{:S(2)}, u32[]{:S(2)}) collective-permute-start(bf16[2,128,128]{2,1,0:T(8,128)(2,1)S(1)} %get-tuple-element.114), channel_id=1, source_target_pairs={{0,4},{4,8},{8,12},{12,0},{1,5},{5,9},{9,13},{13,1},{2,6},{6,10},{... | collective-permute-start | bytes 196616 | tf_op jit(solution)/shard_map/ppermute | solution.py:674
  91.3 4.2 %copy-start.17 = (bf16[2,128,128]{2,1,0:T(8,128)(2,1)}, bf16[2,128,128]{2,1,0:T(8,128)(2,1)S(1)}, u32[]{:S(2)}) copy-start(bf16[2,128,128]{2,1,0:T(8,128)(2,1)S(1)} %collective-permute-done.17.refs_5_) | copy-start | bytes 196612
  94.6 0.9 copy-start.18
  95.4 0.6 copy-start.19
  98.6 6.5 %collective-permute-start.20 = (bf16[2,128,128]{2,1,0:T(8,128)(2,1)}, bf16[2,128,128]{2,1,0:T(8,128)(2,1)S(1)}, u32[]{:S(2)}, u32[]{:S(2)}) collective-permute-start(bf16[2,128,128]{2,1,0:T(8,128)(2,1)} %next_field.1), channel_id=1, source_target_pairs={{0,4},{4,8},{8,12},{12,0},{1,5},{5,9},{9,13},{13,1},{2,6},{6,10},{... | collective-permute-start | bytes 196616 | tf_op jit(solution)/shard_map/ppermute | solution.py:674
  98.6 7.7 %collective-permute-start.19 = (bf16[2,128,128]{2,1,0:T(8,128)(2,1)}, bf16[2,128,128]{2,1,0:T(8,128)(2,1)S(1)}, u32[]{:S(2)}, u32[]{:S(2)}) collective-permute-start(bf16[2,128,128]{2,1,0:T(8,128)(2,1)} %next_field.1), channel_id=1, source_target_pairs={{0,8},{4,12},{8,0},{12,4},{1,9},{5,13},{9,1},{13,5},{2,10},{6,14},... | collective-permute-start | bytes 196616 | tf_op jit(solution)/shard_map/ppermute | solution.py:674
  100.6 5.7 %collective-permute-start.18 = (bf16[2,128,128]{2,1,0:T(8,128)(2,1)}, bf16[2,128,128]{2,1,0:T(8,128)(2,1)S(1)}, u32[]{:S(2)}, u32[]{:S(2)}) collective-permute-start(bf16[2,128,128]{2,1,0:T(8,128)(2,1)} %next_field.1), channel_id=1, source_target_pairs={{0,12},{4,0},{8,4},{12,8},{1,13},{5,1},{9,5},{13,9},{2,14},{6,2},{... | collective-permute-start | bytes 196616 | tf_op jit(solution)/shard_map/ppermute | solution.py:674
  107.2 8.0 %copy-start.5 = (bf16[8,128,128]{2,1,0:T(8,128)(2,1)}, bf16[8,128,128]{2,1,0:T(8,128)(2,1)S(1)}, u32[]{:S(2)}) copy-start(bf16[8,128,128]{2,1,0:T(8,128)(2,1)S(1)} %constant_dynamic-update-slice_fusion.4.refs_0_) | copy-start | bytes 786436
  107.2 6.4 %collective-permute-start.21 = (bf16[8,128,128]{2,1,0:T(8,128)(2,1)S(1)}, bf16[8,128,128]{2,1,0:T(8,128)(2,1)S(1)}, u32[]{:S(2)}, u32[]{:S(2)}) collective-permute-start(bf16[8,128,128]{2,1,0:T(8,128)(2,1)S(1)} %constant_dynamic-update-slice_fusion.4.refs_0_), channel_id=1, source_target_pairs={{0,2},{1,3},{2,0},{3,1},{4,6},{5,7},{6,4},{7,5},{8,10},{9,11},{10,... | collective-permute-start | bytes 786440 | tf_op jit(solution)/shard_map/ppermute | solution.py:669
  108.6 5.1 %collective-permute-start.22 = (bf16[8,128,128]{2,1,0:T(8,128)(2,1)S(1)}, bf16[8,128,128]{2,1,0:T(8,128)(2,1)S(1)}, u32[]{:S(2)}, u32[]{:S(2)}) collective-permute-start(bf16[8,128,128]{2,1,0:T(8,128)(2,1)S(1)} %constant_dynamic-update-slice_fusion.4.refs_0_), channel_id=1, source_target_pairs={{0,1},{1,0},{2,3},{3,2},{4,5},{5,4},{6,7},{7,6},{8,9},{9,8},{10,11... | collective-permute-start | bytes 786440 | tf_op jit(solution)/shard_map/ppermute | solution.py:666
  113.7 1.5 %copy-start.9 = (bf16[8,128,128]{2,1,0:T(8,128)(2,1)}, bf16[8,128,128]{2,1,0:T(8,128)(2,1)S(1)}, u32[]{:S(2)}) copy-start(bf16[8,128,128]{2,1,0:T(8,128)(2,1)S(1)} %collective-permute-done.21.refs_1_) | copy-start | bytes 786436
  113.7 1.5 %collective-permute-start.23 = (bf16[8,128,128]{2,1,0:T(8,128)(2,1)S(1)}, bf16[8,128,128]{2,1,0:T(8,128)(2,1)S(1)}, u32[]{:S(2)}, u32[]{:S(2)}) collective-permute-start(bf16[8,128,128]{2,1,0:T(8,128)(2,1)S(1)} %collective-permute-done.21.refs_1_), channel_id=1, source_target_pairs={{0,1},{1,0},{2,3},{3,2},{4,5},{5,4},{6,7},{7,6},{8,9},{9,8},{10,11... | collective-permute-start | bytes 786440 | tf_op jit(solution)/shard_map/ppermute | solution.py:666
  113.7 1.5 %copy-start.10 = (bf16[8,128,128]{2,1,0:T(8,128)(2,1)}, bf16[8,128,128]{2,1,0:T(8,128)(2,1)S(1)}, u32[]{:S(2)}) copy-start(bf16[8,128,128]{2,1,0:T(8,128)(2,1)S(1)} %collective-permute-done.22.refs_2_) | copy-start | bytes 786436
  115.2 0.7 copy-start.11
where the time goes:
time: 125 us
  Pallas kernels  54 us (43%)
  waiting for transfers between devices  33.7 us (27%)
  starting transfers between devices  26.5 us (21%)
  local copies, waits for them, and re-layouts  5.02 us (4%)
  other arithmetic  4.52 us (4%)
    ppermute x12, starting transfers between devices, to_bin(): lax.ppermute(value, 'bin', [(b, (b + shift) % bins) for b in range(bins)])  19.2 us
    ppermute x5, waiting for transfers between devices, to_chip(): lax.ppermute(value, 'slab', [(s, (s + 2 * shift) % slabs) for s in range(...  17.9 us
    pallas_call x1, Pallas kernels, take_step(): pl.pallas_call(functools.partial(step_kernel, map_side, poses, len(fields...  10.7 us
    pallas_call x1, Pallas kernels, first_projection(): pl.pallas_call(functools.partial(first_projection_kernel, map_side, poses...  10.6 us
    ppermute x12, waiting for transfers between devices, to_bin(): lax.ppermute(value, 'bin', [(b, (b + shift) % bins) for b in range(bins)])  9.72 us
    pallas_call x2, Pallas kernels, table_call(): pl.pallas_call(kernel, grid=(blocks // count,), in_specs=specs, out_specs...  9.26 us
    pallas_call x1, Pallas kernels, finish(): pl.pallas_call(functools.partial(finish_kernel, poses, len(fields)), grid...  8.65 us
    ppermute x7, waiting for transfers between devices, to_core(): return lax.ppermute(value, 'slab', [(s, s ^ 1) for s in range(slabs)])  6.13 us
  transfers between devices with their start and end apart: 24, of which 15 were waited for; matrix products, arithmetic and copies ran while one was open for 2% of the time, Pallas kernels for 16%

commit v1 on v0

--- a/solution.py
+++ b/solution.py
@@ -704,35 +704,50 @@
     keep, send, ctf = image_sums(got_images, defocus, table, pose_count)
     total_parts = reduce_slab(keep, send)
 
-    def share_field(field, early=(), late=()):
+    def share_field(field, meanwhile=()):
         near = [field] + [to_bin(field, bins - d) for d in range(1, bins)]
-        near, early = lax.optimization_barrier((near, early))
         near = jnp.concatenate(near, axis=0)
         across = [to_chip(near, chips - d) for d in range(1, chips)]
-        across, late = lax.optimization_barrier((across, late))
+        across, meanwhile = lax.optimization_barrier((across, meanwhile))
         row = [near] + across
-        return row + [to_core(part) for part in row], early, late
+        return row + [to_core(part) for part in row], meanwhile
+
+    blocks = row_share // BLOCK * (depth // BLOCK)
+    turned = turned_table(wide_geo, blocks, poses, map_side)
 
     field, residual, gains = first_field(proj_parts, total_parts, ctf, table, weight, owned)
-    field, geo, wide_geo = lax.optimization_barrier((field, geo, wide_geo))
-    blocks = row_share // BLOCK * (depth // BLOCK)
-    fields, turned, windows = share_field(
-        field,
-        turned_table(wide_geo, blocks, poses, map_side),
-        window_table(geo, blocks, poses, map_side),
-    )
+    field, geo = lax.optimization_barrier((field, geo))
+    fields, windows = share_field(field, window_table(geo, blocks, poses, map_side))
     start = geo[2]
     first, keep, send = take_step(
         density, fold, fields, start, (windows, turned), step_sizes, bin_index, pool2, pool_t,
         row_share,
     )
-    parts = reduce_slab(keep, send, jnp.bfloat16)
-
-    def change(d):
-        rows = slice(d * owned, (d + 1) * owned)
-        return functools.reduce(jnp.add, [part[rows].astype(jnp.float32) for part in parts])
-
-    moved = [to_bin(change(d).astype(jnp.bfloat16), d) for d in range(1, bins)]
+    got = to_core(send)
+    whole = bins * owned
+
+    def joined(chip_on, low, high):
+        rows = slice(chip_on * whole + low * owned, chip_on * whole + high * owned)
+        return keep[rows] + got[rows].astype(jnp.float32)
+
+    def cross(low, high):
+        return [to_chip(joined(d, low, high).astype(jnp.bfloat16), d) for d in range(1, chips)]
+
+    def block_of(d, low, across):
+        rows = slice((d - low) * owned, (d - low + 1) * owned)
+        value = functools.reduce(
+            jnp.add, [part[rows].astype(jnp.float32) for part in across], joined(0, d, d + 1)
+        )
+        return value.astype(jnp.bfloat16)
+
+    half = bins // 2
+    far = cross(half, bins)
+    near = cross(0, half)
+    leaving = [block_of(d, half, far) for d in range(half, bins)]
+    moved = [to_bin(value, half + k) for k, value in enumerate(leaving)]
+    near, _ = lax.optimization_barrier((near, leaving))
+    moved += [to_bin(block_of(d, 0, near), d) for d in range(1, half)]
+    parts = [keep, got] + near
     field = next_field(parts + moved, residual, gains, table)
     gradient, refined = finish(first, share_field(field)[0], start, turned, step_sizes, pool2)
     return (gradient, refined)

time: 125 us -> 126 us (level)
  other arithmetic: 4.52 us -> 6.18 us
  waiting for transfers between devices: 33.7 us -> 32.3 us
    ppermute x5 -> x6, waiting for transfers between devices: 17.9 us -> 14.9 us  [to_chip(): lax.ppermute(value, 'slab', [(s, (s + 2 * shift) % slabs) for s in range(...]
    ppermute x12, waiting for transfers between devices: 9.72 us -> 12.6 us  [to_bin(): lax.ppermute(value, 'bin', [(b, (b + shift) % bins) for b in range(bins)])]
    ppermute x7, waiting for transfers between devices: 6.13 us -> 4.78 us  [to_core(): return lax.ppermute(value, 'slab', [(s, s ^ 1) for s in range(slabs)])]
    ppermute x5 -> x6, starting transfers between devices: 6.1 us -> 7.06 us  [to_chip(): lax.ppermute(value, 'slab', [(s, (s + 2 * shift) % slabs) for s in range(...]
    convert_element_type x2 -> x3, other arithmetic: 2.48 us -> 3.27 us  [the longest x2 1.99 us: block_of(): return value.astype(jnp.bfloat16)]
    unnamed x48 -> x43, local copies, waits for them, and re-layouts: 4.99 us -> 5.05 us
  transfers between devices with their start and end apart: 24 -> 25, of which waited for: 15 -> 13; matrix products, arithmetic and copies ran while one was open for 2% -> 4% of each run, Pallas kernels for 16% -> 16%
where the time goes in v1:
time: 126 us; the launch traced here: 125 us
  Pallas kernels  54 us (43%)
  waiting for transfers between devices  32.3 us (26%)
  starting transfers between devices  27.1 us (22%)
  other arithmetic  6.18 us (5%)
  local copies, waits for them, and re-layouts  5.07 us (4%)
    ppermute x12, starting transfers between devices, to_bin(): lax.ppermute(value, 'bin', [(b, (b + shift) % bins) for b in range(bins)])  18.8 us
    ppermute x6, waiting for transfers between devices, to_chip(): lax.ppermute(value, 'slab', [(s, (s + 2 * shift) % slabs) for s in range(...  14.9 us
    ppermute x12, waiting for transfers between devices, to_bin(): lax.ppermute(value, 'bin', [(b, (b + shift) % bins) for b in range(bins)])  12.6 us
    pallas_call x1, Pallas kernels, take_step(): pl.pallas_call(functools.partial(step_kernel, map_side, poses, len(fields...  10.7 us
    pallas_call x1, Pallas kernels, first_projection(): pl.pallas_call(functools.partial(first_projection_kernel, map_side, poses...  10.6 us
    pallas_call x2, Pallas kernels, table_call(): pl.pallas_call(kernel, grid=(blocks // count,), in_specs=specs, out_specs...  9.27 us
    pallas_call x1, Pallas kernels, finish(): pl.pallas_call(functools.partial(finish_kernel, poses, len(fields)), grid...  8.66 us
    ppermute x6, starting transfers between devices, to_chip(): lax.ppermute(value, 'slab', [(s, (s + 2 * shift) % slabs) for s in range(...  7.06 us
  transfers between devices with their start and end apart: 25, of which 13 were waited for; matrix products, arithmetic and copies ran while one was open for 4% of the time, Pallas kernels for 16%

profile of v1, /device:TPU:0, one launch (start us, length us, event | category | flops | bytes accessed | tf_op | source)
XLA Modules:
  0.0 125.5 jit_solution(3018007208965760038)
XLA Ops:
  0.6 1.6 %geometry.1 = (f32[8,128]{1,0:T(8,128)}, f32[8,128]{1,0:T(8,128)}, s32[8,128]{1,0:T(8,128)}, f32[8,128]{1,0:T(8,128)}, f32[32,128]{1,0:T(8,128)}, /*index=5*/f32...) custom-call(f32[4,8]{1,0:T(4,128)} %offsets.1), custom_call_target="tpu_custom_call" | custom-call | tf_op jit(solution)/shard_map/geometry/pallas_call | solution.py:177
  2.2 2.2 %pick_images.1 = (bf16[4,144,128]{2,1,0:T(8,128)(2,1)}, bf16[4,144,128]{2,1,0:T(8,128)(2,1)}, bf16[4,144,128]{2,1,0:T(8,128)(2,1)}, bf16[4,144,128]{2,1,0:T(8,128)(2,1)}) custom-call(s32[16]{0:T(128)} %bitcast.2, s32[16]{0:T(128)} %poses_of.1, s32[16]{0:T(128)} %classes_of.1, bf16[16,128,128]{2,1,0:T(8,128)(2,1)} %images.1), custom_call_target="tpu_custom_call" | custom-call | tf_op jit(solution)/shard_map/pick_images/pallas_call | solution.py:360
  4.4 3.1 %collective-permute-start = (bf16[4,144,128]{2,1,0:T(8,128)(2,1)}, bf16[4,144,128]{2,1,0:T(8,128)(2,1)S(1)}, u32[]{:S(2)}, u32[]{:S(2)}) collective-permute-start(bf16[4,144,128]{2,1,0:T(8,128)(2,1)} %get-tuple-element.63), channel_id=1, source_target_pairs={{0,4},{4,8},{8,12},{12,0},{1,5},{5,9},{9,13},{13,1},{2,6},{6,10},{... | collective-permute-start | bytes 442376 | tf_op jit(solution)/shard_map/ppermute | solution.py:674
  7.4 2.6 %collective-permute-start.1 = (bf16[4,144,128]{2,1,0:T(8,128)(2,1)}, bf16[4,144,128]{2,1,0:T(8,128)(2,1)S(1)}, u32[]{:S(2)}, u32[]{:S(2)}) collective-permute-start(bf16[4,144,128]{2,1,0:T(8,128)(2,1)} %get-tuple-element.64), channel_id=1, source_target_pairs={{0,8},{4,12},{8,0},{12,4},{1,9},{5,13},{9,1},{13,5},{2,10},{6,14},... | collective-permute-start | bytes 442376 | tf_op jit(solution)/shard_map/ppermute | solution.py:674
  10.0 1.3 %collective-permute-start.2 = (bf16[4,144,128]{2,1,0:T(8,128)(2,1)}, bf16[4,144,128]{2,1,0:T(8,128)(2,1)S(1)}, u32[]{:S(2)}, u32[]{:S(2)}) collective-permute-start(bf16[4,144,128]{2,1,0:T(8,128)(2,1)} %get-tuple-element.65), channel_id=1, source_target_pairs={{0,12},{4,0},{8,4},{12,8},{1,13},{5,1},{9,5},{13,9},{2,14},{6,2},{... | collective-permute-start | bytes 442376 | tf_op jit(solution)/shard_map/ppermute | solution.py:674
  11.4 10.6 %first_projection.1 = (f32[4,128,128]{2,1,0:T(8,128)}, f32[4,128,128]{2,1,0:T(8,128)}, bf16[256,64,128]{2,1,0:T(8,128)(2,1)}) custom-call(f32[8,128]{1,0:T(8,128)} %get-tuple-element.55.cosine, f32[8,128]{1,0:T(8,128)} %get-tuple-element.56.sine, s32[8,128]{1,0:T(8,128)} %get-tuple-element.57.start, f32[8,128]{1,0:T(8,128)} %get-tuple-element.58.offset, ...), custom_call_target="tpu_custom_call" | custom-call | tf_op jit(solution)/shard_map/first_projection/pallas_call | solution.py:302
  22.0 0.0 collective-permute-done.refs_1_
  22.1 0.0 collective-permute-done.2.refs_3_
  22.1 0.6 copy-done.12
  22.7 0.1 copy-done.13
  22.8 0.7 copy-done.14
  23.4 5.4 %image_sums.1 = (f32[4,136,128]{2,1,0:T(8,128)}, f32[4,136,128]{2,1,0:T(8,128)}, f32[16,128,128]{2,1,0:T(8,128)}) custom-call(f32[16]{0:T(128)} %defocus, bf16[128,256]{1,0:T(8,128)(2,1)} %constant.13.clone.table, bf16[4,144,128]{2,1,0:T(8,128)(2,1)} %get-tuple-element.62.refs_0_, bf16[4,144,128]{2,1,0:T(8,128)(2,1)} %copy-done.12, ...), custom_call_target="tpu_custom_call" | custom-call | tf_op jit(solution)/shard_map/image_sums/pallas_call | solution.py:420
  28.8 0.1 collective-permute-start.5
  28.9 0.5 collective-permute-start.3
  29.4 1.3 %collective-permute-done.5.refs_4_ = f32[4,136,128]{2,1,0:T(8,128)S(1)} collective-permute-done((f32[4,136,128]{2,1,0:T(8,128)}, f32[4,136,128]{2,1,0:T(8,128)S(1)}, u32[]{:S(2)}, u32[]{:S(2)}) %collective-permute-start.5) | collective-permute-done | bytes 278560 | tf_op jit(solution)/shard_map/ppermute | solution.py:666
  30.6 1.0 slice_add_fusion
  31.7 1.6 %collective-permute-start.6 = (f32[2,136,128]{2,1,0:T(8,128)S(1)}, f32[2,136,128]{2,1,0:T(8,128)S(1)}, u32[]{:S(2)}, u32[]{:S(2)}) collective-permute-start(f32[2,136,128]{2,1,0:T(8,128)S(1)} %slice_add_fusion), channel_id=1, source_target_pairs={{0,2},{1,3},{2,0},{3,1},{4,6},{5,7},{6,4},{7,5},{8,10},{9,11},{10,... | collective-permute-start | bytes 417800 | tf_op jit(solution)/shard_map/ppermute | solution.py:669
  33.2 0.0 collective-permute-done.3.refs_1_
  33.2 1.0 slice_add_fusion.1
  34.3 0.6 collective-permute-start.4
  34.8 5.4 %collective-permute-done.4.refs_2_ = f32[2,128,128]{2,1,0:T(8,128)S(1)} collective-permute-done((f32[2,128,128]{2,1,0:T(8,128)S(1)}, f32[2,128,128]{2,1,0:T(8,128)S(1)}, u32[]{:S(2)}, u32[]{:S(2)}) %collective-permute-start.4) | collective-permute-done | bytes 131104 | tf_op jit(solution)/shard_map/ppermute | solution.py:669
  40.3 0.6 copy-done.16
  40.9 0.1 copy-done.15
  41.0 3.0 %first_field.1 = (bf16[2,128,128]{2,1,0:T(8,128)(2,1)}, f32[2,128,128]{2,1,0:T(8,128)}, f32[2,128,128]{2,1,0:T(8,128)}) custom-call(f32[16,128,128]{2,1,0:T(8,128)} %get-tuple-element.66.ctf, bf16[128,256]{1,0:T(8,128)(2,1)} %constant.13.clone.table, f32[4,128,128]{2,1,0:T(8,128)} %get-tuple-element.67.refs_0_, f32[4,128,128]{2,1,0:T(8,128)} %copy-done.3, ...), custom_call_target="tpu_custom_call" | custom-call | tf_op jit(solution)/shard_map/first_field/pallas_call | solution.py:473
  44.0 0.8 collective-permute-start.9
  44.8 2.3 %collective-permute-start.8 = (bf16[2,128,128]{2,1,0:T(8,128)(2,1)}, bf16[2,128,128]{2,1,0:T(8,128)(2,1)S(1)}, u32[]{:S(2)}, u32[]{:S(2)}) collective-permute-start(bf16[2,128,128]{2,1,0:T(8,128)(2,1)} %get-tuple-element.78), channel_id=1, source_target_pairs={{0,8},{4,12},{8,0},{12,4},{1,9},{5,13},{9,1},{13,5},{2,10},{6,14},... | collective-permute-start | bytes 196616 | tf_op jit(solution)/shard_map/ppermute | solution.py:674
  47.1 0.7 collective-permute-start.7
  47.8 0.9 constant_dynamic-update-slice_fusion.3
  48.7 2.9 %collective-permute-done.7 = bf16[2,128,128]{2,1,0:T(8,128)(2,1)S(1)} collective-permute-done((bf16[2,128,128]{2,1,0:T(8,128)(2,1)}, bf16[2,128,128]{2,1,0:T(8,128)(2,1)S(1)}, u32[]{:S(2)}, u32[]{:S(2)}) %collective-permute-start.7) | collective-permute-done | bytes 65568 | tf_op jit(solution)/shard_map/ppermute | solution.py:674
  51.6 0.7 collective-permute-done.8
  52.4 0.0 collective-permute-done.9
  52.4 1.5 %collective-permute-start.10 = (bf16[8,128,128]{2,1,0:T(8,128)(2,1)S(1)}, bf16[8,128,128]{2,1,0:T(8,128)(2,1)S(1)}, u32[]{:S(2)}, u32[]{:S(2)}) collective-permute-start(bf16[8,128,128]{2,1,0:T(8,128)(2,1)S(1)} %constant_dynamic-update-slice_fusion.refs_0_), channel_id=1, source_target_pairs={{0,2},{1,3},{2,0},{3,1},{4,6},{5,7},{6,4},{7,5},{8,10},{9,11},{10,... | collective-permute-start | bytes 786440 | tf_op jit(solution)/shard_map/ppermute | solution.py:669
  53.9 5.2 %shard_map.122.windows = bf16[16,512,256]{2,1,0:T(8,128)(2,1)} custom-call(f32[32,128]{1,0:T(8,128)} %get-tuple-element.79.cosine, f32[32,128]{1,0:T(8,128)} %get-tuple-element.80.sine, s32[32,128]{1,0:T(8,128)} %get-tuple-element.76.start, f32[32,128]{1,0:T(8,128)} %get-tuple-element.81.offset), custom_call_target="tpu_custom_call" | custom-call | tf_op jit(solution)/shard_map/pallas_call | solution.py:234
  59.1 0.5 collective-permute-start.12
  59.6 4.1 %shard_map.123.turned = bf16[16,256,512]{2,1,0:T(8,128)(2,1)} custom-call(f32[2,512]{1,0:T(2,128)} %get-tuple-element.83.wide, f32[16,512]{1,0:T(8,128)} %get-tuple-element.84.lanes), custom_call_target="tpu_custom_call" | custom-call | tf_op jit(solution)/shard_map/pallas_call | solution.py:234
  63.7 0.7 copy-done.7
  64.4 0.1 copy-done.8
  64.5 10.7 %take_step.1 = (f32[64,64,256]{2,1,0:T(8,128)}, f32[16,128,128]{2,1,0:T(8,128)}, bf16[16,128,128]{2,1,0:T(8,128)(2,1)}) custom-call(s32[1]{0:T(128)} %bitcast.1.bin_ref, s32[32,128]{1,0:T(8,128)} %get-tuple-element.76.start, f32[2]{0:T(128)} %sizes.3, bf16[256,64,256]{2,1,0:T(8,128)(2,1)} %dens.3, bf16[256,64,128]{2,1,0:T(8,128)(2,1)} %get-tuple-element.77.fold, ...), custom_call_target="tpu_custom_call" | custom-call | tf_op jit(solution)/shard_map/take_step/pallas_call | solution.py:583
  75.2 0.2 collective-permute-start.13
  75.4 2.0 %collective-permute-done.13.refs_1_ = bf16[16,128,128]{2,1,0:T(8,128)(2,1)S(1)} collective-permute-done((bf16[16,128,128]{2,1,0:T(8,128)(2,1)}, bf16[16,128,128]{2,1,0:T(8,128)(2,1)S(1)}, u32[]{:S(2)}, u32[]{:S(2)}) %collective-permute-start.13) | collective-permute-done | bytes 524320 | tf_op jit(solution)/shard_map/ppermute | solution.py:666
  77.4 1.3 %add_convert_fusion = (bf16[4,128,128]{2,1,0:T(8,128)(2,1)S(1)}, bf16[4,128,128]{2,1,0:T(8,128)(2,1)S(1)}) fusion(f32[16,128,128]{2,1,0:T(8,128)} %get-tuple-element.89.refs_0_, bf16[16,128,128]{2,1,0:T(8,128)(2,1)S(1)} %collective-permute-done.13.refs_1_), kind=kLoop, calls=%fused_computation.1 | loop fusion | flops 393216 | bytes 1048576 | tf_op jit(solution)/shard_map/convert_element_type | solution.py:734
  78.7 0.9 collective-permute-start.15
  79.6 1.2 collective-permute-start.14
  80.8 4.3 %collective-permute-done.15 = bf16[4,128,128]{2,1,0:T(8,128)(2,1)S(1)} collective-permute-done((bf16[4,128,128]{2,1,0:T(8,128)(2,1)S(1)}, bf16[4,128,128]{2,1,0:T(8,128)(2,1)S(1)}, u32[]{:S(2)}, u32[]{:S(2)}) %collective-permute-start.15) | collective-permute-done | bytes 131104 | tf_op jit(solution)/shard_map/ppermute | solution.py:669
  85.1 1.0 add_convert_fusion.3
  86.1 3.5 %collective-permute-start.17 = (bf16[2,128,128]{2,1,0:T(8,128)(2,1)S(1)}, bf16[2,128,128]{2,1,0:T(8,128)(2,1)S(1)}, u32[]{:S(2)}, u32[]{:S(2)}) collective-permute-start(bf16[2,128,128]{2,1,0:T(8,128)(2,1)S(1)} %get-tuple-element.92), channel_id=1, source_target_pairs={{0,12},{4,0},{8,4},{12,8},{1,13},{5,1},{9,5},{13,9},{2,14},{6,2},{... | collective-permute-start | bytes 196616 | tf_op jit(solution)/shard_map/ppermute | solution.py:674
  89.6 0.4 collective-permute-start.16
  90.0 1.0 add_convert_fusion.2
  91.0 0.3 collective-permute-start.18
  91.3 0.5 collective-permute-done.17.refs_4_
  91.8 3.4 %collective-permute-done.16.refs_3_ = bf16[2,128,128]{2,1,0:T(8,128)(2,1)S(1)} collective-permute-done((bf16[2,128,128]{2,1,0:T(8,128)(2,1)S(1)}, bf16[2,128,128]{2,1,0:T(8,128)(2,1)S(1)}, u32[]{:S(2)}, u32[]{:S(2)}) %collective-permute-start.16) | collective-permute-done | bytes 65568 | tf_op jit(solution)/shard_map/ppermute | solution.py:674
  95.2 1.9 %collective-permute-done.18.refs_5_ = bf16[2,128,128]{2,1,0:T(8,128)(2,1)S(1)} collective-permute-done((bf16[2,128,128]{2,1,0:T(8,128)(2,1)S(1)}, bf16[2,128,128]{2,1,0:T(8,128)(2,1)S(1)}, u32[]{:S(2)}, u32[]{:S(2)}) %collective-permute-start.18) | collective-permute-done | bytes 65568 | tf_op jit(solution)/shard_map/ppermute | solution.py:674
  97.2 0.6 copy-done.19
  97.8 2.5 %next_field.1 = bf16[2,128,128]{2,1,0:T(8,128)(2,1)} custom-call(bf16[128,256]{1,0:T(8,128)(2,1)} %constant.13.clone.table, f32[2,128,128]{2,1,0:T(8,128)} %get-tuple-element.87.residual, f32[2,128,128]{2,1,0:T(8,128)} %get-tuple-element.88.gains, f32[16,128,128]{2,1,0:T(8,128)} %get-tuple-element.89.refs_0_, bf16[16,128,128]{2,1,0:T(8,128)(2,1)} %copy-done, ...), custom_call_target="tpu_custom_call" | custom-call | tf_op jit(solution)/shard_map/next_field/pallas_call | solution.py:494
  100.3 0.7 collective-permute-start.20
  101.0 3.1 %collective-permute-start.19 = (bf16[2,128,128]{2,1,0:T(8,128)(2,1)}, bf16[2,128,128]{2,1,0:T(8,128)(2,1)S(1)}, u32[]{:S(2)}, u32[]{:S(2)}) collective-permute-start(bf16[2,128,128]{2,1,0:T(8,128)(2,1)} %next_field.1), channel_id=1, source_target_pairs={{0,12},{4,0},{8,4},{12,8},{1,13},{5,1},{9,5},{13,9},{2,14},{6,2},{... | collective-permute-start | bytes 196616 | tf_op jit(solution)/shard_map/ppermute | solution.py:674
  104.1 2.5 %collective-permute-done.21 = bf16[2,128,128]{2,1,0:T(8,128)(2,1)S(1)} collective-permute-done((bf16[2,128,128]{2,1,0:T(8,128)(2,1)}, bf16[2,128,128]{2,1,0:T(8,128)(2,1)S(1)}, u32[]{:S(2)}, u32[]{:S(2)}) %collective-permute-start.21) | collective-permute-done | bytes 65568 | tf_op jit(solution)/shard_map/ppermute | solution.py:674
  106.6 0.7 collective-permute-done.19
  107.3 0.9 pad_maximum_fusion.refs_0_
  108.2 1.3 %collective-permute-start.22 = (bf16[8,128,128]{2,1,0:T(8,128)(2,1)S(1)}, bf16[8,128,128]{2,1,0:T(8,128)(2,1)S(1)}, u32[]{:S(2)}, u32[]{:S(2)}) collective-permute-start(bf16[8,128,128]{2,1,0:T(8,128)(2,1)S(1)} %pad_maximum_fusion.refs_0_), channel_id=1, source_target_pairs={{0,2},{1,3},{2,0},{3,1},{4,6},{5,7},{6,4},{7,5},{8,10},{9,11},{10,... | collective-permute-start | bytes 786440 | tf_op jit(solution)/shard_map/ppermute | solution.py:669
  109.5 5.1 %collective-permute-done.22.refs_1_ = bf16[8,128,128]{2,1,0:T(8,128)(2,1)S(1)} collective-permute-done((bf16[8,128,128]{2,1,0:T(8,128)(2,1)S(1)}, bf16[8,128,128]{2,1,0:T(8,128)(2,1)S(1)}, u32[]{:S(2)}, u32[]{:S(2)}) %collective-permute-start.22) | collective-permute-done | bytes 262176 | tf_op jit(solution)/shard_map/ppermute | solution.py:669
  114.6 1.5 %collective-permute-done.24.refs_3_ = bf16[8,128,128]{2,1,0:T(8,128)(2,1)S(1)} collective-permute-done((bf16[8,128,128]{2,1,0:T(8,128)(2,1)S(1)}, bf16[8,128,128]{2,1,0:T(8,128)(2,1)S(1)}, u32[]{:S(2)}, u32[]{:S(2)}) %collective-permute-start.24) | collective-permute-done | bytes 262176 | tf_op jit(solution)/shard_map/ppermute | solution.py:666
  116.1 0.7 copy-done.11
  116.8 8.7 %finish.1 = (f32[64,64,256]{2,1,0:T(8,128)}, f32[64,64,256]{2,1,0:T(8,128)}) custom-call(s32[32,128]{1,0:T(8,128)} %get-tuple-element.76.start, f32[2]{0:T(128)} %sizes.3, f32[64,64,256]{2,1,0:T(8,128)} %get-tuple-element.86.first, bf16[16,256,512]{2,1,0:T(8,128)(2,1)} %shard_map.123.turned, bf16[256,256]{1,0:T(8,128)(2,1)} %constant.12.clone.pool2, ...), custom_call_target="tpu_custom_call" | custom-call | tf_op jit(solution)/shard_map/finish/pallas_call | solution.py:634
  (46 shorter events, 0.1 us)
Async XLA Ops:
  4.4 17.6 %collective-permute-start = (bf16[4,144,128]{2,1,0:T(8,128)(2,1)}, bf16[4,144,128]{2,1,0:T(8,128)(2,1)S(1)}, u32[]{:S(2)}, u32[]{:S(2)}) collective-permute-start(bf16[4,144,128]{2,1,0:T(8,128)(2,1)} %get-tuple-element.63), channel_id=1, source_target_pairs={{0,4},{4,8},{8,12},{12,0},{1,5},{5,9},{9,13},{13,1},{2,6},{6,10},{... | collective-permute-start | bytes 442376 | tf_op jit(solution)/shard_map/ppermute | solution.py:674
  7.4 14.6 %collective-permute-start.1 = (bf16[4,144,128]{2,1,0:T(8,128)(2,1)}, bf16[4,144,128]{2,1,0:T(8,128)(2,1)S(1)}, u32[]{:S(2)}, u32[]{:S(2)}) collective-permute-start(bf16[4,144,128]{2,1,0:T(8,128)(2,1)} %get-tuple-element.64), channel_id=1, source_target_pairs={{0,8},{4,12},{8,0},{12,4},{1,9},{5,13},{9,1},{13,5},{2,10},{6,14},... | collective-permute-start | bytes 442376 | tf_op jit(solution)/shard_map/ppermute | solution.py:674
  10.0 12.0 %collective-permute-start.2 = (bf16[4,144,128]{2,1,0:T(8,128)(2,1)}, bf16[4,144,128]{2,1,0:T(8,128)(2,1)S(1)}, u32[]{:S(2)}, u32[]{:S(2)}) collective-permute-start(bf16[4,144,128]{2,1,0:T(8,128)(2,1)} %get-tuple-element.65), channel_id=1, source_target_pairs={{0,12},{4,0},{8,4},{12,8},{1,13},{5,1},{9,5},{13,9},{2,14},{6,2},{... | collective-permute-start | bytes 442376 | tf_op jit(solution)/shard_map/ppermute | solution.py:674
  22.0 0.7 copy-start.12
  22.1 0.7 copy-start.13
  22.8 0.7 copy-start.14
  28.8 1.8 %collective-permute-start.5 = (f32[4,136,128]{2,1,0:T(8,128)}, f32[4,136,128]{2,1,0:T(8,128)S(1)}, u32[]{:S(2)}, u32[]{:S(2)}) collective-permute-start(f32[4,136,128]{2,1,0:T(8,128)} %get-tuple-element.70), channel_id=1, source_target_pairs={{0,1},{1,0},{2,3},{3,2},{4,5},{5,4},{6,7},{7,6},{8,9},{9,8},{10,11... | collective-permute-start | bytes 835592 | tf_op jit(solution)/shard_map/ppermute | solution.py:666
  28.9 4.4 %collective-permute-start.3 = (f32[4,128,128]{2,1,0:T(8,128)}, f32[4,128,128]{2,1,0:T(8,128)S(1)}, u32[]{:S(2)}, u32[]{:S(2)}) collective-permute-start(f32[4,128,128]{2,1,0:T(8,128)} %get-tuple-element.68), channel_id=1, source_target_pairs={{0,1},{1,0},{2,3},{3,2},{4,5},{5,4},{6,7},{7,6},{8,9},{9,8},{10,11... | collective-permute-start | bytes 786440 | tf_op jit(solution)/shard_map/ppermute | solution.py:666
  30.6 9.6 %copy-start.2 = (f32[4,136,128]{2,1,0:T(8,128)}, f32[4,136,128]{2,1,0:T(8,128)S(1)}, u32[]{:S(2)}) copy-start(f32[4,136,128]{2,1,0:T(8,128)S(1)} %collective-permute-done.5.refs_4_) | copy-start | bytes 835588
  31.7 8.6 %collective-permute-start.6 = (f32[2,136,128]{2,1,0:T(8,128)S(1)}, f32[2,136,128]{2,1,0:T(8,128)S(1)}, u32[]{:S(2)}, u32[]{:S(2)}) collective-permute-start(f32[2,136,128]{2,1,0:T(8,128)S(1)} %slice_add_fusion), channel_id=1, source_target_pairs={{0,2},{1,3},{2,0},{3,1},{4,6},{5,7},{6,4},{7,5},{8,10},{9,11},{10,... | collective-permute-start | bytes 417800 | tf_op jit(solution)/shard_map/ppermute | solution.py:669
  33.2 7.0 %copy-start.3 = (f32[4,128,128]{2,1,0:T(8,128)}, f32[4,128,128]{2,1,0:T(8,128)S(1)}, u32[]{:S(2)}) copy-start(f32[4,128,128]{2,1,0:T(8,128)S(1)} %collective-permute-done.3.refs_1_) | copy-start | bytes 786436
  34.3 6.0 %collective-permute-start.4 = (f32[2,128,128]{2,1,0:T(8,128)S(1)}, f32[2,128,128]{2,1,0:T(8,128)S(1)}, u32[]{:S(2)}, u32[]{:S(2)}) collective-permute-start(f32[2,128,128]{2,1,0:T(8,128)S(1)} %slice_add_fusion.1), channel_id=1, source_target_pairs={{0,2},{1,3},{2,0},{3,1},{4,6},{5,7},{6,4},{7,5},{8,10},{9,11},{10,... | collective-permute-start | bytes 393224 | tf_op jit(solution)/shard_map/ppermute | solution.py:669
  40.3 0.7 copy-start.16
  40.3 0.7 copy-start.15
  44.0 8.4 %collective-permute-start.9 = (bf16[2,128,128]{2,1,0:T(8,128)(2,1)}, bf16[2,128,128]{2,1,0:T(8,128)(2,1)S(1)}, u32[]{:S(2)}, u32[]{:S(2)}) collective-permute-start(bf16[2,128,128]{2,1,0:T(8,128)(2,1)} %get-tuple-element.78), channel_id=1, source_target_pairs={{0,4},{4,8},{8,12},{12,0},{1,5},{5,9},{9,13},{13,1},{2,6},{6,10},{... | collective-permute-start | bytes 196616 | tf_op jit(solution)/shard_map/ppermute | solution.py:674
  44.8 7.5 %collective-permute-start.8 = (bf16[2,128,128]{2,1,0:T(8,128)(2,1)}, bf16[2,128,128]{2,1,0:T(8,128)(2,1)S(1)}, u32[]{:S(2)}, u32[]{:S(2)}) collective-permute-start(bf16[2,128,128]{2,1,0:T(8,128)(2,1)} %get-tuple-element.78), channel_id=1, source_target_pairs={{0,8},{4,12},{8,0},{12,4},{1,9},{5,13},{9,1},{13,5},{2,10},{6,14},... | collective-permute-start | bytes 196616 | tf_op jit(solution)/shard_map/ppermute | solution.py:674
  47.1 4.5 %collective-permute-start.7 = (bf16[2,128,128]{2,1,0:T(8,128)(2,1)}, bf16[2,128,128]{2,1,0:T(8,128)(2,1)S(1)}, u32[]{:S(2)}, u32[]{:S(2)}) collective-permute-start(bf16[2,128,128]{2,1,0:T(8,128)(2,1)} %get-tuple-element.78), channel_id=1, source_target_pairs={{0,12},{4,0},{8,4},{12,8},{1,13},{5,1},{9,5},{13,9},{2,14},{6,2},{... | collective-permute-start | bytes 196616 | tf_op jit(solution)/shard_map/ppermute | solution.py:674
  52.4 11.3 %copy-start.4 = (bf16[8,128,128]{2,1,0:T(8,128)(2,1)}, bf16[8,128,128]{2,1,0:T(8,128)(2,1)S(1)}, u32[]{:S(2)}) copy-start(bf16[8,128,128]{2,1,0:T(8,128)(2,1)S(1)} %constant_dynamic-update-slice_fusion.refs_0_) | copy-start | bytes 786436
  52.4 6.7 %collective-permute-start.10 = (bf16[8,128,128]{2,1,0:T(8,128)(2,1)S(1)}, bf16[8,128,128]{2,1,0:T(8,128)(2,1)S(1)}, u32[]{:S(2)}, u32[]{:S(2)}) collective-permute-start(bf16[8,128,128]{2,1,0:T(8,128)(2,1)S(1)} %constant_dynamic-update-slice_fusion.refs_0_), channel_id=1, source_target_pairs={{0,2},{1,3},{2,0},{3,1},{4,6},{5,7},{6,4},{7,5},{8,10},{9,11},{10,... | collective-permute-start | bytes 786440 | tf_op jit(solution)/shard_map/ppermute | solution.py:669
  59.1 4.6 %collective-permute-start.11 = (bf16[8,128,128]{2,1,0:T(8,128)(2,1)S(1)}, bf16[8,128,128]{2,1,0:T(8,128)(2,1)S(1)}, u32[]{:S(2)}, u32[]{:S(2)}) collective-permute-start(bf16[8,128,128]{2,1,0:T(8,128)(2,1)S(1)} %constant_dynamic-update-slice_fusion.refs_0_), channel_id=1, source_target_pairs={{0,1},{1,0},{2,3},{3,2},{4,5},{5,4},{6,7},{7,6},{8,9},{9,8},{10,11... | collective-permute-start | bytes 786440 | tf_op jit(solution)/shard_map/ppermute | solution.py:666
  59.1 4.6 %copy-start.6 = (bf16[8,128,128]{2,1,0:T(8,128)(2,1)}, bf16[8,128,128]{2,1,0:T(8,128)(2,1)S(1)}, u32[]{:S(2)}) copy-start(bf16[8,128,128]{2,1,0:T(8,128)(2,1)S(1)} %collective-permute-done.10.refs_1_) | copy-start | bytes 786436
  59.1 4.6 %collective-permute-start.12 = (bf16[8,128,128]{2,1,0:T(8,128)(2,1)S(1)}, bf16[8,128,128]{2,1,0:T(8,128)(2,1)S(1)}, u32[]{:S(2)}, u32[]{:S(2)}) collective-permute-start(bf16[8,128,128]{2,1,0:T(8,128)(2,1)S(1)} %collective-permute-done.10.refs_1_), channel_id=1, source_target_pairs={{0,1},{1,0},{2,3},{3,2},{4,5},{5,4},{6,7},{7,6},{8,9},{9,8},{10,11... | collective-permute-start | bytes 786440 | tf_op jit(solution)/shard_map/ppermute | solution.py:666
  63.7 0.7 copy-start.7
  63.7 0.8 copy-start.8
  75.2 2.2 %collective-permute-start.13 = (bf16[16,128,128]{2,1,0:T(8,128)(2,1)}, bf16[16,128,128]{2,1,0:T(8,128)(2,1)S(1)}, u32[]{:S(2)}, u32[]{:S(2)}) collective-permute-start(bf16[16,128,128]{2,1,0:T(8,128)(2,1)} %get-tuple-element.90), channel_id=1, source_target_pairs={{0,1},{1,0},{2,3},{3,2},{4,5},{5,4},{6,7},{7,6},{8,9},{9,8},{10,11... | collective-permute-start | bytes 1572872 | tf_op jit(solution)/shard_map/ppermute | solution.py:666
  77.4 19.7 %copy-start = (bf16[16,128,128]{2,1,0:T(8,128)(2,1)}, bf16[16,128,128]{2,1,0:T(8,128)(2,1)S(1)}, u32[]{:S(2)}) copy-start(bf16[16,128,128]{2,1,0:T(8,128)(2,1)S(1)} %collective-permute-done.13.refs_1_) | copy-start | bytes 1572868
  78.7 6.4 %collective-permute-start.15 = (bf16[4,128,128]{2,1,0:T(8,128)(2,1)S(1)}, bf16[4,128,128]{2,1,0:T(8,128)(2,1)S(1)}, u32[]{:S(2)}, u32[]{:S(2)}) collective-permute-start(bf16[4,128,128]{2,1,0:T(8,128)(2,1)S(1)} %get-tuple-element.94), channel_id=1, source_target_pairs={{0,2},{1,3},{2,0},{3,1},{4,6},{5,7},{6,4},{7,5},{8,10},{9,11},{10,... | collective-permute-start | bytes 393224 | tf_op jit(solution)/shard_map/ppermute | solution.py:669
  79.6 10.5 %collective-permute-start.14 = (bf16[4,128,128]{2,1,0:T(8,128)(2,1)S(1)}, bf16[4,128,128]{2,1,0:T(8,128)(2,1)S(1)}, u32[]{:S(2)}, u32[]{:S(2)}) collective-permute-start(bf16[4,128,128]{2,1,0:T(8,128)(2,1)S(1)} %get-tuple-element.95), channel_id=1, source_target_pairs={{0,2},{1,3},{2,0},{3,1},{4,6},{5,7},{6,4},{7,5},{8,10},{9,11},{10,... | collective-permute-start | bytes 393224 | tf_op jit(solution)/shard_map/ppermute | solution.py:669
  86.1 5.6 %collective-permute-start.17 = (bf16[2,128,128]{2,1,0:T(8,128)(2,1)S(1)}, bf16[2,128,128]{2,1,0:T(8,128)(2,1)S(1)}, u32[]{:S(2)}, u32[]{:S(2)}) collective-permute-start(bf16[2,128,128]{2,1,0:T(8,128)(2,1)S(1)} %get-tuple-element.92), channel_id=1, source_target_pairs={{0,12},{4,0},{8,4},{12,8},{1,13},{5,1},{9,5},{13,9},{2,14},{6,2},{... | collective-permute-start | bytes 196616 | tf_op jit(solution)/shard_map/ppermute | solution.py:674
  89.6 5.6 %collective-permute-start.16 = (bf16[2,128,128]{2,1,0:T(8,128)(2,1)S(1)}, bf16[2,128,128]{2,1,0:T(8,128)(2,1)S(1)}, u32[]{:S(2)}, u32[]{:S(2)}) collective-permute-start(bf16[2,128,128]{2,1,0:T(8,128)(2,1)S(1)} %get-tuple-element.93), channel_id=1, source_target_pairs={{0,8},{4,12},{8,0},{12,4},{1,9},{5,13},{9,1},{13,5},{2,10},{6,14},... | collective-permute-start | bytes 196616 | tf_op jit(solution)/shard_map/ppermute | solution.py:674
  90.0 7.1 %copy-start.5 = (bf16[4,128,128]{2,1,0:T(8,128)(2,1)}, bf16[4,128,128]{2,1,0:T(8,128)(2,1)S(1)}, u32[]{:S(2)}) copy-start(bf16[4,128,128]{2,1,0:T(8,128)(2,1)S(1)} %collective-permute-done.14.refs_2_) | copy-start | bytes 393220
  91.0 6.1 %collective-permute-start.18 = (bf16[2,128,128]{2,1,0:T(8,128)(2,1)S(1)}, bf16[2,128,128]{2,1,0:T(8,128)(2,1)S(1)}, u32[]{:S(2)}, u32[]{:S(2)}) collective-permute-start(bf16[2,128,128]{2,1,0:T(8,128)(2,1)S(1)} %add_convert_fusion.2), channel_id=1, source_target_pairs={{0,4},{4,8},{8,12},{12,0},{1,5},{5,9},{9,13},{13,1},{2,6},{6,10},{... | collective-permute-start | bytes 196616 | tf_op jit(solution)/shard_map/ppermute | solution.py:674
  91.8 5.4 %copy-start.17 = (bf16[2,128,128]{2,1,0:T(8,128)(2,1)}, bf16[2,128,128]{2,1,0:T(8,128)(2,1)S(1)}, u32[]{:S(2)}) copy-start(bf16[2,128,128]{2,1,0:T(8,128)(2,1)S(1)} %collective-permute-done.17.refs_4_) | copy-start | bytes 196612
  95.2 1.9 %copy-start.18 = (bf16[2,128,128]{2,1,0:T(8,128)(2,1)}, bf16[2,128,128]{2,1,0:T(8,128)(2,1)S(1)}, u32[]{:S(2)}) copy-start(bf16[2,128,128]{2,1,0:T(8,128)(2,1)S(1)} %collective-permute-done.16.refs_3_) | copy-start | bytes 196612
  97.1 0.6 copy-start.19
  100.3 6.3 %collective-permute-start.21 = (bf16[2,128,128]{2,1,0:T(8,128)(2,1)}, bf16[2,128,128]{2,1,0:T(8,128)(2,1)S(1)}, u32[]{:S(2)}, u32[]{:S(2)}) collective-permute-start(bf16[2,128,128]{2,1,0:T(8,128)(2,1)} %next_field.1), channel_id=1, source_target_pairs={{0,4},{4,8},{8,12},{12,0},{1,5},{5,9},{9,13},{13,1},{2,6},{6,10},{... | collective-permute-start | bytes 196616 | tf_op jit(solution)/shard_map/ppermute | solution.py:674
  100.3 6.3 %collective-permute-start.20 = (bf16[2,128,128]{2,1,0:T(8,128)(2,1)}, bf16[2,128,128]{2,1,0:T(8,128)(2,1)S(1)}, u32[]{:S(2)}, u32[]{:S(2)}) collective-permute-start(bf16[2,128,128]{2,1,0:T(8,128)(2,1)} %next_field.1), channel_id=1, source_target_pairs={{0,8},{4,12},{8,0},{12,4},{1,9},{5,13},{9,1},{13,5},{2,10},{6,14},... | collective-permute-start | bytes 196616 | tf_op jit(solution)/shard_map/ppermute | solution.py:674
  101.0 6.3 %collective-permute-start.19 = (bf16[2,128,128]{2,1,0:T(8,128)(2,1)}, bf16[2,128,128]{2,1,0:T(8,128)(2,1)S(1)}, u32[]{:S(2)}, u32[]{:S(2)}) collective-permute-start(bf16[2,128,128]{2,1,0:T(8,128)(2,1)} %next_field.1), channel_id=1, source_target_pairs={{0,12},{4,0},{8,4},{12,8},{1,13},{5,1},{9,5},{13,9},{2,14},{6,2},{... | collective-permute-start | bytes 196616 | tf_op jit(solution)/shard_map/ppermute | solution.py:674
  108.1 8.0 %copy-start.1 = (bf16[8,128,128]{2,1,0:T(8,128)(2,1)}, bf16[8,128,128]{2,1,0:T(8,128)(2,1)S(1)}, u32[]{:S(2)}) copy-start(bf16[8,128,128]{2,1,0:T(8,128)(2,1)S(1)} %pad_maximum_fusion.refs_0_) | copy-start | bytes 786436
  108.2 6.4 %collective-permute-start.22 = (bf16[8,128,128]{2,1,0:T(8,128)(2,1)S(1)}, bf16[8,128,128]{2,1,0:T(8,128)(2,1)S(1)}, u32[]{:S(2)}, u32[]{:S(2)}) collective-permute-start(bf16[8,128,128]{2,1,0:T(8,128)(2,1)S(1)} %pad_maximum_fusion.refs_0_), channel_id=1, source_target_pairs={{0,2},{1,3},{2,0},{3,1},{4,6},{5,7},{6,4},{7,5},{8,10},{9,11},{10,... | collective-permute-start | bytes 786440 | tf_op jit(solution)/shard_map/ppermute | solution.py:669
  109.5 5.1 %collective-permute-start.23 = (bf16[8,128,128]{2,1,0:T(8,128)(2,1)S(1)}, bf16[8,128,128]{2,1,0:T(8,128)(2,1)S(1)}, u32[]{:S(2)}, u32[]{:S(2)}) collective-permute-start(bf16[8,128,128]{2,1,0:T(8,128)(2,1)S(1)} %pad_maximum_fusion.refs_0_), channel_id=1, source_target_pairs={{0,1},{1,0},{2,3},{3,2},{4,5},{5,4},{6,7},{7,6},{8,9},{9,8},{10,11... | collective-permute-start | bytes 786440 | tf_op jit(solution)/shard_map/ppermute | solution.py:666
  114.6 1.5 %copy-start.9 = (bf16[8,128,128]{2,1,0:T(8,128)(2,1)}, bf16[8,128,128]{2,1,0:T(8,128)(2,1)S(1)}, u32[]{:S(2)}) copy-start(bf16[8,128,128]{2,1,0:T(8,128)(2,1)S(1)} %collective-permute-done.22.refs_1_) | copy-start | bytes 786436
  114.6 1.5 %collective-permute-start.24 = (bf16[8,128,128]{2,1,0:T(8,128)(2,1)S(1)}, bf16[8,128,128]{2,1,0:T(8,128)(2,1)S(1)}, u32[]{:S(2)}, u32[]{:S(2)}) collective-permute-start(bf16[8,128,128]{2,1,0:T(8,128)(2,1)S(1)} %collective-permute-done.22.refs_1_), channel_id=1, source_target_pairs={{0,1},{1,0},{2,3},{3,2},{4,5},{5,4},{6,7},{7,6},{8,9},{9,8},{10,11... | collective-permute-start | bytes 786440 | tf_op jit(solution)/shard_map/ppermute | solution.py:666
  114.6 1.5 %copy-start.10 = (bf16[8,128,128]{2,1,0:T(8,128)(2,1)}, bf16[8,128,128]{2,1,0:T(8,128)(2,1)S(1)}, u32[]{:S(2)}) copy-start(bf16[8,128,128]{2,1,0:T(8,128)(2,1)S(1)} %collective-permute-done.23.refs_2_) | copy-start | bytes 786436
  116.1 0.7 copy-start.11

commit v2 on v1

--- a/solution.py
+++ b/solution.py
@@ -297,7 +297,7 @@
 def first_projection(density, pool_t, geo, poses):
     map_side, depth, _ = density.shape
     side = pool_t.shape[1]
-    height = 2 * BLOCK
+    height = 4 * BLOCK
     half = jax.ShapeDtypeStruct((poses // 2, side, side), jnp.float32)
     return pl.pallas_call(
         functools.partial(first_projection_kernel, map_side, poses),
@@ -704,20 +704,23 @@
     keep, send, ctf = image_sums(got_images, defocus, table, pose_count)
     total_parts = reduce_slab(keep, send)
 
-    def share_field(field, meanwhile=()):
+    def share_field(field, early=(), late=()):
         near = [field] + [to_bin(field, bins - d) for d in range(1, bins)]
+        near, early = lax.optimization_barrier((near, early))
         near = jnp.concatenate(near, axis=0)
         across = [to_chip(near, chips - d) for d in range(1, chips)]
-        across, meanwhile = lax.optimization_barrier((across, meanwhile))
+        across, late = lax.optimization_barrier((across, late))
         row = [near] + across
-        return row + [to_core(part) for part in row], meanwhile
-
+        return row + [to_core(part) for part in row], early, late
+
+    field, residual, gains = first_field(proj_parts, total_parts, ctf, table, weight, owned)
+    field, geo, wide_geo = lax.optimization_barrier((field, geo, wide_geo))
     blocks = row_share // BLOCK * (depth // BLOCK)
-    turned = turned_table(wide_geo, blocks, poses, map_side)
-
-    field, residual, gains = first_field(proj_parts, total_parts, ctf, table, weight, owned)
-    field, geo = lax.optimization_barrier((field, geo))
-    fields, windows = share_field(field, window_table(geo, blocks, poses, map_side))
+    fields, turned, windows = share_field(
+        field,
+        turned_table(wide_geo, blocks, poses, map_side),
+        window_table(geo, blocks, poses, map_side),
+    )
     start = geo[2]
     first, keep, send = take_step(
         density, fold, fields, start, (windows, turned), step_sizes, bin_index, pool2, pool_t,

time: 126 us -> 123 us (0.976)
  Pallas kernels: 54 us -> 52.3 us
    ppermute x12, waiting for transfers between devices: 12.6 us -> 9.86 us  [to_bin(): lax.ppermute(value, 'bin', [(b, (b + shift) % bins) for b in range(bins)])]
    pallas_call x1, Pallas kernels: 10.6 us -> 8.97 us  [first_projection(): pl.pallas_call(functools.partial(first_projection_kernel, map_side, poses...]
    ppermute x7, waiting for transfers between devices: 4.78 us -> 6.27 us  [to_core(): return lax.ppermute(value, 'slab', [(s, s ^ 1) for s in range(slabs)])]
    unnamed x43 -> x48, local copies, waits for them, and re-layouts: 5.05 us -> 4.96 us
  transfers between devices with their start and end apart: 25 -> 25, of which waited for: 13 -> 16; matrix products, arithmetic and copies ran while one was open for 4% -> 3% of each run, Pallas kernels for 16% -> 15%
where the time goes in v2:
time: 123 us; the launch traced here: 122 us
  Pallas kernels  52.3 us (43%)
  waiting for transfers between devices  31.7 us (26%)
  starting transfers between devices  27.1 us (22%)
  other arithmetic  5.31 us (4%)
  local copies, waits for them, and re-layouts  4.99 us (4%)
    ppermute x12, starting transfers between devices, to_bin(): lax.ppermute(value, 'bin', [(b, (b + shift) % bins) for b in range(bins)])  19.3 us
    ppermute x6, waiting for transfers between devices, to_chip(): lax.ppermute(value, 'slab', [(s, (s + 2 * shift) % slabs) for s in range(...  15.5 us
    pallas_call x1, Pallas kernels, take_step(): pl.pallas_call(functools.partial(step_kernel, map_side, poses, len(fields...  10.7 us
    ppermute x12, waiting for transfers between devices, to_bin(): lax.ppermute(value, 'bin', [(b, (b + shift) % bins) for b in range(bins)])  9.86 us
    pallas_call x2, Pallas kernels, table_call(): pl.pallas_call(kernel, grid=(blocks // count,), in_specs=specs, out_specs...  9.28 us
    pallas_call x1, Pallas kernels, first_projection(): pl.pallas_call(functools.partial(first_projection_kernel, map_side, poses...  8.97 us
    pallas_call x1, Pallas kernels, finish(): pl.pallas_call(functools.partial(finish_kernel, poses, len(fields)), grid...  8.65 us
    ppermute x6, starting transfers between devices, to_chip(): lax.ppermute(value, 'slab', [(s, (s + 2 * shift) % slabs) for s in range(...  7.06 us
  transfers between devices with their start and end apart: 25, of which 16 were waited for; matrix products, arithmetic and copies ran while one was open for 3% of the time, Pallas kernels for 15%

profile of v2, /device:TPU:0, one launch (start us, length us, event | category | flops | bytes accessed | tf_op | source)
XLA Modules:
  0.0 122.3 jit_solution(10173493002665035600)
XLA Ops:
  0.6 1.6 %geometry.1 = (f32[8,128]{1,0:T(8,128)}, f32[8,128]{1,0:T(8,128)}, s32[8,128]{1,0:T(8,128)}, f32[8,128]{1,0:T(8,128)}, f32[32,128]{1,0:T(8,128)}, /*index=5*/f32...) custom-call(f32[4,8]{1,0:T(4,128)} %offsets.1), custom_call_target="tpu_custom_call" | custom-call | tf_op jit(solution)/shard_map/geometry/pallas_call | solution.py:177
  2.2 2.2 %pick_images.1 = (bf16[4,144,128]{2,1,0:T(8,128)(2,1)}, bf16[4,144,128]{2,1,0:T(8,128)(2,1)}, bf16[4,144,128]{2,1,0:T(8,128)(2,1)}, bf16[4,144,128]{2,1,0:T(8,128)(2,1)}) custom-call(s32[16]{0:T(128)} %bitcast.2, s32[16]{0:T(128)} %poses_of.1, s32[16]{0:T(128)} %classes_of.1, bf16[16,128,128]{2,1,0:T(8,128)(2,1)} %images.1), custom_call_target="tpu_custom_call" | custom-call | tf_op jit(solution)/shard_map/pick_images/pallas_call | solution.py:360
  4.4 3.1 %collective-permute-start = (bf16[4,144,128]{2,1,0:T(8,128)(2,1)}, bf16[4,144,128]{2,1,0:T(8,128)(2,1)S(1)}, u32[]{:S(2)}, u32[]{:S(2)}) collective-permute-start(bf16[4,144,128]{2,1,0:T(8,128)(2,1)} %get-tuple-element.74), channel_id=1, source_target_pairs={{0,4},{4,8},{8,12},{12,0},{1,5},{5,9},{9,13},{13,1},{2,6},{6,10},{... | collective-permute-start | bytes 442376 | tf_op jit(solution)/shard_map/ppermute | solution.py:674
  7.4 2.6 %collective-permute-start.1 = (bf16[4,144,128]{2,1,0:T(8,128)(2,1)}, bf16[4,144,128]{2,1,0:T(8,128)(2,1)S(1)}, u32[]{:S(2)}, u32[]{:S(2)}) collective-permute-start(bf16[4,144,128]{2,1,0:T(8,128)(2,1)} %get-tuple-element.75), channel_id=1, source_target_pairs={{0,8},{4,12},{8,0},{12,4},{1,9},{5,13},{9,1},{13,5},{2,10},{6,14},... | collective-permute-start | bytes 442376 | tf_op jit(solution)/shard_map/ppermute | solution.py:674
  10.0 1.3 %collective-permute-start.2 = (bf16[4,144,128]{2,1,0:T(8,128)(2,1)}, bf16[4,144,128]{2,1,0:T(8,128)(2,1)S(1)}, u32[]{:S(2)}, u32[]{:S(2)}) collective-permute-start(bf16[4,144,128]{2,1,0:T(8,128)(2,1)} %get-tuple-element.76), channel_id=1, source_target_pairs={{0,12},{4,0},{8,4},{12,8},{1,13},{5,1},{9,5},{13,9},{2,14},{6,2},{... | collective-permute-start | bytes 442376 | tf_op jit(solution)/shard_map/ppermute | solution.py:674
  11.4 9.0 %first_projection.1 = (f32[4,128,128]{2,1,0:T(8,128)}, f32[4,128,128]{2,1,0:T(8,128)}, bf16[256,64,128]{2,1,0:T(8,128)(2,1)}) custom-call(f32[8,128]{1,0:T(8,128)} %get-tuple-element.66.cosine, f32[8,128]{1,0:T(8,128)} %get-tuple-element.67.sine, s32[8,128]{1,0:T(8,128)} %get-tuple-element.68.start, f32[8,128]{1,0:T(8,128)} %get-tuple-element.69.offset, ...), custom_call_target="tpu_custom_call" | custom-call | tf_op jit(solution)/shard_map/first_projection/pallas_call | solution.py:302
  20.4 0.0 collective-permute-done.2.refs_3_
  20.4 0.6 copy-done.12
  21.0 0.1 copy-done.13
  21.1 0.7 copy-done.14
  21.8 5.4 %image_sums.1 = (f32[4,136,128]{2,1,0:T(8,128)}, f32[4,136,128]{2,1,0:T(8,128)}, f32[16,128,128]{2,1,0:T(8,128)}) custom-call(f32[16]{0:T(128)} %defocus, bf16[128,256]{1,0:T(8,128)(2,1)} %constant.13.clone.table, bf16[4,144,128]{2,1,0:T(8,128)(2,1)} %get-tuple-element.73.refs_0_, bf16[4,144,128]{2,1,0:T(8,128)(2,1)} %copy-done.12, ...), custom_call_target="tpu_custom_call" | custom-call | tf_op jit(solution)/shard_map/image_sums/pallas_call | solution.py:420
  27.1 0.1 collective-permute-start.5
  27.2 0.5 collective-permute-start.3
  27.7 1.3 %collective-permute-done.5.refs_4_ = f32[4,136,128]{2,1,0:T(8,128)S(1)} collective-permute-done((f32[4,136,128]{2,1,0:T(8,128)}, f32[4,136,128]{2,1,0:T(8,128)S(1)}, u32[]{:S(2)}, u32[]{:S(2)}) %collective-permute-start.5) | collective-permute-done | bytes 278560 | tf_op jit(solution)/shard_map/ppermute | solution.py:666
  29.0 1.0 slice_add_fusion
  30.0 1.6 %collective-permute-start.6 = (f32[2,136,128]{2,1,0:T(8,128)S(1)}, f32[2,136,128]{2,1,0:T(8,128)S(1)}, u32[]{:S(2)}, u32[]{:S(2)}) collective-permute-start(f32[2,136,128]{2,1,0:T(8,128)S(1)} %slice_add_fusion), channel_id=1, source_target_pairs={{0,2},{1,3},{2,0},{3,1},{4,6},{5,7},{6,4},{7,5},{8,10},{9,11},{10,... | collective-permute-start | bytes 417800 | tf_op jit(solution)/shard_map/ppermute | solution.py:669
  31.5 1.0 slice_add_fusion.1
  32.6 0.6 collective-permute-start.4
  33.2 5.4 %collective-permute-done.4.refs_2_ = f32[2,128,128]{2,1,0:T(8,128)S(1)} collective-permute-done((f32[2,128,128]{2,1,0:T(8,128)S(1)}, f32[2,128,128]{2,1,0:T(8,128)S(1)}, u32[]{:S(2)}, u32[]{:S(2)}) %collective-permute-start.4) | collective-permute-done | bytes 131104 | tf_op jit(solution)/shard_map/ppermute | solution.py:669
  38.6 0.0 collective-permute-done.6.refs_5_
  38.6 0.6 copy-done.16
  39.2 0.0 copy-done.15
  39.3 3.0 %first_field.1 = (bf16[2,128,128]{2,1,0:T(8,128)(2,1)}, f32[2,128,128]{2,1,0:T(8,128)}, f32[2,128,128]{2,1,0:T(8,128)}) custom-call(f32[16,128,128]{2,1,0:T(8,128)} %get-tuple-element.77.ctf, bf16[128,256]{1,0:T(8,128)(2,1)} %constant.13.clone.table, f32[4,128,128]{2,1,0:T(8,128)} %get-tuple-element.78.refs_0_, f32[4,128,128]{2,1,0:T(8,128)} %copy-done.2, ...), custom_call_target="tpu_custom_call" | custom-call | tf_op jit(solution)/shard_map/first_field/pallas_call | solution.py:473
  42.3 2.5 %collective-permute-start.9 = (bf16[2,128,128]{2,1,0:T(8,128)(2,1)}, bf16[2,128,128]{2,1,0:T(8,128)(2,1)S(1)}, u32[]{:S(2)}, u32[]{:S(2)}) collective-permute-start(bf16[2,128,128]{2,1,0:T(8,128)(2,1)} %get-tuple-element.94), channel_id=1, source_target_pairs={{0,4},{4,8},{8,12},{12,0},{1,5},{5,9},{9,13},{13,1},{2,6},{6,10},{... | collective-permute-start | bytes 196616 | tf_op jit(solution)/shard_map/ppermute | solution.py:674
  44.8 2.3 %collective-permute-start.8 = (bf16[2,128,128]{2,1,0:T(8,128)(2,1)}, bf16[2,128,128]{2,1,0:T(8,128)(2,1)S(1)}, u32[]{:S(2)}, u32[]{:S(2)}) collective-permute-start(bf16[2,128,128]{2,1,0:T(8,128)(2,1)} %get-tuple-element.94), channel_id=1, source_target_pairs={{0,8},{4,12},{8,0},{12,4},{1,9},{5,13},{9,1},{13,5},{2,10},{6,14},... | collective-permute-start | bytes 196616 | tf_op jit(solution)/shard_map/ppermute | solution.py:674
  47.1 0.2 collective-permute-start.7
  47.2 4.1 %shard_map.122.turned = bf16[16,256,512]{2,1,0:T(8,128)(2,1)} custom-call(f32[2,512]{1,0:T(2,128)} %get-tuple-element.92.wide, f32[16,512]{1,0:T(8,128)} %get-tuple-element.93.lanes), custom_call_target="tpu_custom_call" | custom-call | tf_op jit(solution)/shard_map/pallas_call | solution.py:234
  51.3 0.0 collective-permute-done.9
  51.3 0.3 collective-permute-done.8
  51.6 0.4 collective-permute-done.7
  52.1 1.5 %collective-permute-start.10 = (bf16[8,128,128]{2,1,0:T(8,128)(2,1)S(1)}, bf16[8,128,128]{2,1,0:T(8,128)(2,1)S(1)}, u32[]{:S(2)}, u32[]{:S(2)}) collective-permute-start(bf16[8,128,128]{2,1,0:T(8,128)(2,1)S(1)} %constant_dynamic-update-slice_fusion.refs_0_), channel_id=1, source_target_pairs={{0,2},{1,3},{2,0},{3,1},{4,6},{5,7},{6,4},{7,5},{8,10},{9,11},{10,... | collective-permute-start | bytes 786440 | tf_op jit(solution)/shard_map/ppermute | solution.py:669
  53.5 5.2 %shard_map.123.windows = bf16[16,512,256]{2,1,0:T(8,128)(2,1)} custom-call(f32[32,128]{1,0:T(8,128)} %get-tuple-element.98.cosine, f32[32,128]{1,0:T(8,128)} %get-tuple-element.99.sine, s32[32,128]{1,0:T(8,128)} %get-tuple-element.89.start, f32[32,128]{1,0:T(8,128)} %get-tuple-element.100.offset), custom_call_target="tpu_custom_call" | custom-call | tf_op jit(solution)/shard_map/pallas_call | solution.py:234
  58.7 0.7 collective-permute-done.10.refs_1_
  59.4 0.0 collective-permute-start.12
  59.4 0.8 collective-permute-done.11.refs_2_
  60.3 0.7 collective-permute-done.12.refs_3_
  61.0 0.7 copy-done.8
  61.7 10.7 %take_step.1 = (f32[64,64,256]{2,1,0:T(8,128)}, f32[16,128,128]{2,1,0:T(8,128)}, bf16[16,128,128]{2,1,0:T(8,128)(2,1)}) custom-call(s32[1]{0:T(128)} %bitcast.1.bin_ref, s32[32,128]{1,0:T(8,128)} %get-tuple-element.89.start, f32[2]{0:T(128)} %sizes.3, bf16[256,64,256]{2,1,0:T(8,128)(2,1)} %dens.3, bf16[256,64,128]{2,1,0:T(8,128)(2,1)} %get-tuple-element.90.fold, ...), custom_call_target="tpu_custom_call" | custom-call | tf_op jit(solution)/shard_map/take_step/pallas_call | solution.py:583
  72.4 0.2 collective-permute-start.13
  72.6 2.0 %collective-permute-done.13.refs_1_ = bf16[16,128,128]{2,1,0:T(8,128)(2,1)S(1)} collective-permute-done((bf16[16,128,128]{2,1,0:T(8,128)(2,1)}, bf16[16,128,128]{2,1,0:T(8,128)(2,1)S(1)}, u32[]{:S(2)}, u32[]{:S(2)}) %collective-permute-start.13) | collective-permute-done | bytes 524320 | tf_op jit(solution)/shard_map/ppermute | solution.py:666
  74.6 1.3 %add_convert_fusion = (bf16[4,128,128]{2,1,0:T(8,128)(2,1)S(1)}, bf16[4,128,128]{2,1,0:T(8,128)(2,1)S(1)}) fusion(f32[16,128,128]{2,1,0:T(8,128)} %get-tuple-element.107.refs_0_, bf16[16,128,128]{2,1,0:T(8,128)(2,1)S(1)} %collective-permute-done.13.refs_1_), kind=kLoop, calls=%fused_computation | loop fusion | flops 393216 | bytes 1048576 | tf_op jit(solution)/shard_map/convert_element_type | solution.py:737
  75.9 1.4 %collective-permute-start.15 = (bf16[4,128,128]{2,1,0:T(8,128)(2,1)S(1)}, bf16[4,128,128]{2,1,0:T(8,128)(2,1)S(1)}, u32[]{:S(2)}, u32[]{:S(2)}) collective-permute-start(bf16[4,128,128]{2,1,0:T(8,128)(2,1)S(1)} %get-tuple-element.116), channel_id=1, source_target_pairs={{0,2},{1,3},{2,0},{3,1},{4,6},{5,7},{6,4},{7,5},{8,10},{9,11},{10,... | collective-permute-start | bytes 393224 | tf_op jit(solution)/shard_map/ppermute | solution.py:669
  77.2 0.7 collective-permute-start.14
  78.0 4.3 %collective-permute-done.15 = bf16[4,128,128]{2,1,0:T(8,128)(2,1)S(1)} collective-permute-done((bf16[4,128,128]{2,1,0:T(8,128)(2,1)S(1)}, bf16[4,128,128]{2,1,0:T(8,128)(2,1)S(1)}, u32[]{:S(2)}, u32[]{:S(2)}) %collective-permute-start.15) | collective-permute-done | bytes 131104 | tf_op jit(solution)/shard_map/ppermute | solution.py:669
  82.3 1.0 add_convert_fusion.3
  83.3 2.3 %collective-permute-start.17 = (bf16[2,128,128]{2,1,0:T(8,128)(2,1)S(1)}, bf16[2,128,128]{2,1,0:T(8,128)(2,1)S(1)}, u32[]{:S(2)}, u32[]{:S(2)}) collective-permute-start(bf16[2,128,128]{2,1,0:T(8,128)(2,1)S(1)} %get-tuple-element.114), channel_id=1, source_target_pairs={{0,12},{4,0},{8,4},{12,8},{1,13},{5,1},{9,5},{13,9},{2,14},{6,2},{... | collective-permute-start | bytes 196616 | tf_op jit(solution)/shard_map/ppermute | solution.py:674
  85.6 1.2 collective-permute-start.16
  86.8 1.0 add_convert_fusion.2
  87.8 0.1 collective-permute-start.18
  87.9 0.5 collective-permute-done.17.refs_4_
  88.4 3.2 %collective-permute-done.16.refs_3_ = bf16[2,128,128]{2,1,0:T(8,128)(2,1)S(1)} collective-permute-done((bf16[2,128,128]{2,1,0:T(8,128)(2,1)S(1)}, bf16[2,128,128]{2,1,0:T(8,128)(2,1)S(1)}, u32[]{:S(2)}, u32[]{:S(2)}) %collective-permute-start.16) | collective-permute-done | bytes 65568 | tf_op jit(solution)/shard_map/ppermute | solution.py:674
  91.5 2.4 %collective-permute-done.18.refs_5_ = bf16[2,128,128]{2,1,0:T(8,128)(2,1)S(1)} collective-permute-done((bf16[2,128,128]{2,1,0:T(8,128)(2,1)S(1)}, bf16[2,128,128]{2,1,0:T(8,128)(2,1)S(1)}, u32[]{:S(2)}, u32[]{:S(2)}) %collective-permute-start.18) | collective-permute-done | bytes 65568 | tf_op jit(solution)/shard_map/ppermute | solution.py:674
  94.0 0.6 copy-done.19
  94.6 2.5 %next_field.1 = bf16[2,128,128]{2,1,0:T(8,128)(2,1)} custom-call(bf16[128,256]{1,0:T(8,128)(2,1)} %constant.13.clone.table, f32[2,128,128]{2,1,0:T(8,128)} %get-tuple-element.105.residual, f32[2,128,128]{2,1,0:T(8,128)} %get-tuple-element.106.gains, f32[16,128,128]{2,1,0:T(8,128)} %get-tuple-element.107.refs_0_, bf16[16,128,128]{2,1,0:T(8,128)(2,1)} %copy-done, ...), custom_call_target="tpu_custom_call" | custom-call | tf_op jit(solution)/shard_map/next_field/pallas_call | solution.py:494
  97.1 0.2 collective-permute-start.20
  97.3 3.6 %collective-permute-start.19 = (bf16[2,128,128]{2,1,0:T(8,128)(2,1)}, bf16[2,128,128]{2,1,0:T(8,128)(2,1)S(1)}, u32[]{:S(2)}, u32[]{:S(2)}) collective-permute-start(bf16[2,128,128]{2,1,0:T(8,128)(2,1)} %next_field.1), channel_id=1, source_target_pairs={{0,12},{4,0},{8,4},{12,8},{1,13},{5,1},{9,5},{13,9},{2,14},{6,2},{... | collective-permute-start | bytes 196616 | tf_op jit(solution)/shard_map/ppermute | solution.py:674
  100.9 2.5 %collective-permute-done.21 = bf16[2,128,128]{2,1,0:T(8,128)(2,1)S(1)} collective-permute-done((bf16[2,128,128]{2,1,0:T(8,128)(2,1)}, bf16[2,128,128]{2,1,0:T(8,128)(2,1)S(1)}, u32[]{:S(2)}, u32[]{:S(2)}) %collective-permute-start.21) | collective-permute-done | bytes 65568 | tf_op jit(solution)/shard_map/ppermute | solution.py:674
  103.4 0.7 collective-permute-done.19
  104.1 0.8 constant_dynamic-update-slice_fusion.7
  105.0 1.3 %collective-permute-start.22 = (bf16[8,128,128]{2,1,0:T(8,128)(2,1)S(1)}, bf16[8,128,128]{2,1,0:T(8,128)(2,1)S(1)}, u32[]{:S(2)}, u32[]{:S(2)}) collective-permute-start(bf16[8,128,128]{2,1,0:T(8,128)(2,1)S(1)} %constant_dynamic-update-slice_fusion.4.refs_0_), channel_id=1, source_target_pairs={{0,2},{1,3},{2,0},{3,1},{4,6},{5,7},{6,4},{7,5},{8,10},{9,11},{10,... | collective-permute-start | bytes 786440 | tf_op jit(solution)/shard_map/ppermute | solution.py:669
  106.3 5.1 %collective-permute-done.22.refs_1_ = bf16[8,128,128]{2,1,0:T(8,128)(2,1)S(1)} collective-permute-done((bf16[8,128,128]{2,1,0:T(8,128)(2,1)S(1)}, bf16[8,128,128]{2,1,0:T(8,128)(2,1)S(1)}, u32[]{:S(2)}, u32[]{:S(2)}) %collective-permute-start.22) | collective-permute-done | bytes 262176 | tf_op jit(solution)/shard_map/ppermute | solution.py:669
  111.4 1.5 %collective-permute-done.24.refs_3_ = bf16[8,128,128]{2,1,0:T(8,128)(2,1)S(1)} collective-permute-done((bf16[8,128,128]{2,1,0:T(8,128)(2,1)S(1)}, bf16[8,128,128]{2,1,0:T(8,128)(2,1)S(1)}, u32[]{:S(2)}, u32[]{:S(2)}) %collective-permute-start.24) | collective-permute-done | bytes 262176 | tf_op jit(solution)/shard_map/ppermute | solution.py:666
  113.0 0.7 copy-done.11
  113.6 8.6 %finish.1 = (f32[64,64,256]{2,1,0:T(8,128)}, f32[64,64,256]{2,1,0:T(8,128)}) custom-call(s32[32,128]{1,0:T(8,128)} %get-tuple-element.89.start, f32[2]{0:T(128)} %sizes.3, f32[64,64,256]{2,1,0:T(8,128)} %get-tuple-element.104.first, bf16[16,256,512]{2,1,0:T(8,128)(2,1)} %shard_map.122.turned, bf16[256,256]{1,0:T(8,128)(2,1)} %constant.12.clone.pool2, ...), custom_call_target="tpu_custom_call" | custom-call | tf_op jit(solution)/shard_map/finish/pallas_call | solution.py:634
  (51 shorter events, 0.2 us)
Async XLA Ops:
  4.4 16.0 %collective-permute-start = (bf16[4,144,128]{2,1,0:T(8,128)(2,1)}, bf16[4,144,128]{2,1,0:T(8,128)(2,1)S(1)}, u32[]{:S(2)}, u32[]{:S(2)}) collective-permute-start(bf16[4,144,128]{2,1,0:T(8,128)(2,1)} %get-tuple-element.74), channel_id=1, source_target_pairs={{0,4},{4,8},{8,12},{12,0},{1,5},{5,9},{9,13},{13,1},{2,6},{6,10},{... | collective-permute-start | bytes 442376 | tf_op jit(solution)/shard_map/ppermute | solution.py:674
  7.4 12.9 %collective-permute-start.1 = (bf16[4,144,128]{2,1,0:T(8,128)(2,1)}, bf16[4,144,128]{2,1,0:T(8,128)(2,1)S(1)}, u32[]{:S(2)}, u32[]{:S(2)}) collective-permute-start(bf16[4,144,128]{2,1,0:T(8,128)(2,1)} %get-tuple-element.75), channel_id=1, source_target_pairs={{0,8},{4,12},{8,0},{12,4},{1,9},{5,13},{9,1},{13,5},{2,10},{6,14},... | collective-permute-start | bytes 442376 | tf_op jit(solution)/shard_map/ppermute | solution.py:674
  10.0 10.4 %collective-permute-start.2 = (bf16[4,144,128]{2,1,0:T(8,128)(2,1)}, bf16[4,144,128]{2,1,0:T(8,128)(2,1)S(1)}, u32[]{:S(2)}, u32[]{:S(2)}) collective-permute-start(bf16[4,144,128]{2,1,0:T(8,128)(2,1)} %get-tuple-element.76), channel_id=1, source_target_pairs={{0,12},{4,0},{8,4},{12,8},{1,13},{5,1},{9,5},{13,9},{2,14},{6,2},{... | collective-permute-start | bytes 442376 | tf_op jit(solution)/shard_map/ppermute | solution.py:674
  20.4 0.7 copy-start.12
  20.4 0.7 copy-start.13
  21.1 0.7 copy-start.14
  27.1 1.8 %collective-permute-start.5 = (f32[4,136,128]{2,1,0:T(8,128)}, f32[4,136,128]{2,1,0:T(8,128)S(1)}, u32[]{:S(2)}, u32[]{:S(2)}) collective-permute-start(f32[4,136,128]{2,1,0:T(8,128)} %get-tuple-element.81), channel_id=1, source_target_pairs={{0,1},{1,0},{2,3},{3,2},{4,5},{5,4},{6,7},{7,6},{8,9},{9,8},{10,11... | collective-permute-start | bytes 835592 | tf_op jit(solution)/shard_map/ppermute | solution.py:666
  27.2 4.3 %collective-permute-start.3 = (f32[4,128,128]{2,1,0:T(8,128)}, f32[4,128,128]{2,1,0:T(8,128)S(1)}, u32[]{:S(2)}, u32[]{:S(2)}) collective-permute-start(f32[4,128,128]{2,1,0:T(8,128)} %get-tuple-element.79), channel_id=1, source_target_pairs={{0,1},{1,0},{2,3},{3,2},{4,5},{5,4},{6,7},{7,6},{8,9},{9,8},{10,11... | collective-permute-start | bytes 786440 | tf_op jit(solution)/shard_map/ppermute | solution.py:666
  29.0 9.6 %copy-start.1 = (f32[4,136,128]{2,1,0:T(8,128)}, f32[4,136,128]{2,1,0:T(8,128)S(1)}, u32[]{:S(2)}) copy-start(f32[4,136,128]{2,1,0:T(8,128)S(1)} %collective-permute-done.5.refs_4_) | copy-start | bytes 835588
  30.0 8.6 %collective-permute-start.6 = (f32[2,136,128]{2,1,0:T(8,128)S(1)}, f32[2,136,128]{2,1,0:T(8,128)S(1)}, u32[]{:S(2)}, u32[]{:S(2)}) collective-permute-start(f32[2,136,128]{2,1,0:T(8,128)S(1)} %slice_add_fusion), channel_id=1, source_target_pairs={{0,2},{1,3},{2,0},{3,1},{4,6},{5,7},{6,4},{7,5},{8,10},{9,11},{10,... | collective-permute-start | bytes 417800 | tf_op jit(solution)/shard_map/ppermute | solution.py:669
  31.5 7.0 %copy-start.2 = (f32[4,128,128]{2,1,0:T(8,128)}, f32[4,128,128]{2,1,0:T(8,128)S(1)}, u32[]{:S(2)}) copy-start(f32[4,128,128]{2,1,0:T(8,128)S(1)} %collective-permute-done.3.refs_1_) | copy-start | bytes 786436
  32.6 6.0 %collective-permute-start.4 = (f32[2,128,128]{2,1,0:T(8,128)S(1)}, f32[2,128,128]{2,1,0:T(8,128)S(1)}, u32[]{:S(2)}, u32[]{:S(2)}) collective-permute-start(f32[2,128,128]{2,1,0:T(8,128)S(1)} %slice_add_fusion.1), channel_id=1, source_target_pairs={{0,2},{1,3},{2,0},{3,1},{4,6},{5,7},{6,4},{7,5},{8,10},{9,11},{10,... | collective-permute-start | bytes 393224 | tf_op jit(solution)/shard_map/ppermute | solution.py:669
  38.6 0.7 copy-start.16
  38.6 0.7 copy-start.15
  42.3 9.7 %copy-start.20 = (bf16[2,128,128]{2,1,0:T(8,128)(2,1)S(1)}, bf16[2,128,128]{2,1,0:T(8,128)(2,1)}, u32[]{:S(2)}) copy-start(bf16[2,128,128]{2,1,0:T(8,128)(2,1)} %get-tuple-element.94) | copy-start | bytes 196612
  42.3 9.0 %collective-permute-start.9 = (bf16[2,128,128]{2,1,0:T(8,128)(2,1)}, bf16[2,128,128]{2,1,0:T(8,128)(2,1)S(1)}, u32[]{:S(2)}, u32[]{:S(2)}) collective-permute-start(bf16[2,128,128]{2,1,0:T(8,128)(2,1)} %get-tuple-element.94), channel_id=1, source_target_pairs={{0,4},{4,8},{8,12},{12,0},{1,5},{5,9},{9,13},{13,1},{2,6},{6,10},{... | collective-permute-start | bytes 196616 | tf_op jit(solution)/shard_map/ppermute | solution.py:674
  44.8 6.8 %collective-permute-start.8 = (bf16[2,128,128]{2,1,0:T(8,128)(2,1)}, bf16[2,128,128]{2,1,0:T(8,128)(2,1)S(1)}, u32[]{:S(2)}, u32[]{:S(2)}) collective-permute-start(bf16[2,128,128]{2,1,0:T(8,128)(2,1)} %get-tuple-element.94), channel_id=1, source_target_pairs={{0,8},{4,12},{8,0},{12,4},{1,9},{5,13},{9,1},{13,5},{2,10},{6,14},... | collective-permute-start | bytes 196616 | tf_op jit(solution)/shard_map/ppermute | solution.py:674
  47.1 4.9 %collective-permute-start.7 = (bf16[2,128,128]{2,1,0:T(8,128)(2,1)}, bf16[2,128,128]{2,1,0:T(8,128)(2,1)S(1)}, u32[]{:S(2)}, u32[]{:S(2)}) collective-permute-start(bf16[2,128,128]{2,1,0:T(8,128)(2,1)} %get-tuple-element.94), channel_id=1, source_target_pairs={{0,12},{4,0},{8,4},{12,8},{1,13},{5,1},{9,5},{13,9},{2,14},{6,2},{... | collective-permute-start | bytes 196616 | tf_op jit(solution)/shard_map/ppermute | solution.py:674
  52.1 8.9 %copy-start.3 = (bf16[8,128,128]{2,1,0:T(8,128)(2,1)}, bf16[8,128,128]{2,1,0:T(8,128)(2,1)S(1)}, u32[]{:S(2)}) copy-start(bf16[8,128,128]{2,1,0:T(8,128)(2,1)S(1)} %constant_dynamic-update-slice_fusion.refs_0_) | copy-start | bytes 786436
  52.1 7.4 %collective-permute-start.10 = (bf16[8,128,128]{2,1,0:T(8,128)(2,1)S(1)}, bf16[8,128,128]{2,1,0:T(8,128)(2,1)S(1)}, u32[]{:S(2)}, u32[]{:S(2)}) collective-permute-start(bf16[8,128,128]{2,1,0:T(8,128)(2,1)S(1)} %constant_dynamic-update-slice_fusion.refs_0_), channel_id=1, source_target_pairs={{0,2},{1,3},{2,0},{3,1},{4,6},{5,7},{6,4},{7,5},{8,10},{9,11},{10,... | collective-permute-start | bytes 786440 | tf_op jit(solution)/shard_map/ppermute | solution.py:669
  58.7 1.5 %collective-permute-start.11 = (bf16[8,128,128]{2,1,0:T(8,128)(2,1)S(1)}, bf16[8,128,128]{2,1,0:T(8,128)(2,1)S(1)}, u32[]{:S(2)}, u32[]{:S(2)}) collective-permute-start(bf16[8,128,128]{2,1,0:T(8,128)(2,1)S(1)} %constant_dynamic-update-slice_fusion.refs_0_), channel_id=1, source_target_pairs={{0,1},{1,0},{2,3},{3,2},{4,5},{5,4},{6,7},{7,6},{8,9},{9,8},{10,11... | collective-permute-start | bytes 786440 | tf_op jit(solution)/shard_map/ppermute | solution.py:666
  59.4 1.5 %copy-start.6 = (bf16[8,128,128]{2,1,0:T(8,128)(2,1)}, bf16[8,128,128]{2,1,0:T(8,128)(2,1)S(1)}, u32[]{:S(2)}) copy-start(bf16[8,128,128]{2,1,0:T(8,128)(2,1)S(1)} %collective-permute-done.10.refs_1_) | copy-start | bytes 786436
  59.4 1.5 %collective-permute-start.12 = (bf16[8,128,128]{2,1,0:T(8,128)(2,1)S(1)}, bf16[8,128,128]{2,1,0:T(8,128)(2,1)S(1)}, u32[]{:S(2)}, u32[]{:S(2)}) collective-permute-start(bf16[8,128,128]{2,1,0:T(8,128)(2,1)S(1)} %collective-permute-done.10.refs_1_), channel_id=1, source_target_pairs={{0,1},{1,0},{2,3},{3,2},{4,5},{5,4},{6,7},{7,6},{8,9},{9,8},{10,11... | collective-permute-start | bytes 786440 | tf_op jit(solution)/shard_map/ppermute | solution.py:666
  60.3 0.7 copy-start.7
  61.0 0.7 copy-start.8
  72.4 2.2 %collective-permute-start.13 = (bf16[16,128,128]{2,1,0:T(8,128)(2,1)}, bf16[16,128,128]{2,1,0:T(8,128)(2,1)S(1)}, u32[]{:S(2)}, u32[]{:S(2)}) collective-permute-start(bf16[16,128,128]{2,1,0:T(8,128)(2,1)} %get-tuple-element.108), channel_id=1, source_target_pairs={{0,1},{1,0},{2,3},{3,2},{4,5},{5,4},{6,7},{7,6},{8,9},{9,8},{10,11... | collective-permute-start | bytes 1572872 | tf_op jit(solution)/shard_map/ppermute | solution.py:666
  74.6 19.3 %copy-start = (bf16[16,128,128]{2,1,0:T(8,128)(2,1)}, bf16[16,128,128]{2,1,0:T(8,128)(2,1)S(1)}, u32[]{:S(2)}) copy-start(bf16[16,128,128]{2,1,0:T(8,128)(2,1)S(1)} %collective-permute-done.13.refs_1_) | copy-start | bytes 1572868
  75.9 6.4 %collective-permute-start.15 = (bf16[4,128,128]{2,1,0:T(8,128)(2,1)S(1)}, bf16[4,128,128]{2,1,0:T(8,128)(2,1)S(1)}, u32[]{:S(2)}, u32[]{:S(2)}) collective-permute-start(bf16[4,128,128]{2,1,0:T(8,128)(2,1)S(1)} %get-tuple-element.116), channel_id=1, source_target_pairs={{0,2},{1,3},{2,0},{3,1},{4,6},{5,7},{6,4},{7,5},{8,10},{9,11},{10,... | collective-permute-start | bytes 393224 | tf_op jit(solution)/shard_map/ppermute | solution.py:669
  77.2 9.6 %collective-permute-start.14 = (bf16[4,128,128]{2,1,0:T(8,128)(2,1)S(1)}, bf16[4,128,128]{2,1,0:T(8,128)(2,1)S(1)}, u32[]{:S(2)}, u32[]{:S(2)}) collective-permute-start(bf16[4,128,128]{2,1,0:T(8,128)(2,1)S(1)} %get-tuple-element.117), channel_id=1, source_target_pairs={{0,2},{1,3},{2,0},{3,1},{4,6},{5,7},{6,4},{7,5},{8,10},{9,11},{10,... | collective-permute-start | bytes 393224 | tf_op jit(solution)/shard_map/ppermute | solution.py:669
  83.3 5.0 %collective-permute-start.17 = (bf16[2,128,128]{2,1,0:T(8,128)(2,1)S(1)}, bf16[2,128,128]{2,1,0:T(8,128)(2,1)S(1)}, u32[]{:S(2)}, u32[]{:S(2)}) collective-permute-start(bf16[2,128,128]{2,1,0:T(8,128)(2,1)S(1)} %get-tuple-element.114), channel_id=1, source_target_pairs={{0,12},{4,0},{8,4},{12,8},{1,13},{5,1},{9,5},{13,9},{2,14},{6,2},{... | collective-permute-start | bytes 196616 | tf_op jit(solution)/shard_map/ppermute | solution.py:674
  85.6 5.9 %collective-permute-start.16 = (bf16[2,128,128]{2,1,0:T(8,128)(2,1)S(1)}, bf16[2,128,128]{2,1,0:T(8,128)(2,1)S(1)}, u32[]{:S(2)}, u32[]{:S(2)}) collective-permute-start(bf16[2,128,128]{2,1,0:T(8,128)(2,1)S(1)} %get-tuple-element.115), channel_id=1, source_target_pairs={{0,8},{4,12},{8,0},{12,4},{1,9},{5,13},{9,1},{13,5},{2,10},{6,14},... | collective-permute-start | bytes 196616 | tf_op jit(solution)/shard_map/ppermute | solution.py:674
  86.8 7.1 %copy-start.5 = (bf16[4,128,128]{2,1,0:T(8,128)(2,1)}, bf16[4,128,128]{2,1,0:T(8,128)(2,1)S(1)}, u32[]{:S(2)}) copy-start(bf16[4,128,128]{2,1,0:T(8,128)(2,1)S(1)} %collective-permute-done.14.refs_2_) | copy-start | bytes 393220
  87.8 6.1 %collective-permute-start.18 = (bf16[2,128,128]{2,1,0:T(8,128)(2,1)S(1)}, bf16[2,128,128]{2,1,0:T(8,128)(2,1)S(1)}, u32[]{:S(2)}, u32[]{:S(2)}) collective-permute-start(bf16[2,128,128]{2,1,0:T(8,128)(2,1)S(1)} %add_convert_fusion.2), channel_id=1, source_target_pairs={{0,4},{4,8},{8,12},{12,0},{1,5},{5,9},{9,13},{13,1},{2,6},{6,10},{... | collective-permute-start | bytes 196616 | tf_op jit(solution)/shard_map/ppermute | solution.py:674
  88.4 5.6 %copy-start.17 = (bf16[2,128,128]{2,1,0:T(8,128)(2,1)}, bf16[2,128,128]{2,1,0:T(8,128)(2,1)S(1)}, u32[]{:S(2)}) copy-start(bf16[2,128,128]{2,1,0:T(8,128)(2,1)S(1)} %collective-permute-done.17.refs_4_) | copy-start | bytes 196612
  91.5 2.4 %copy-start.18 = (bf16[2,128,128]{2,1,0:T(8,128)(2,1)}, bf16[2,128,128]{2,1,0:T(8,128)(2,1)S(1)}, u32[]{:S(2)}) copy-start(bf16[2,128,128]{2,1,0:T(8,128)(2,1)S(1)} %collective-permute-done.16.refs_3_) | copy-start | bytes 196612
  93.9 0.6 copy-start.19
  97.1 6.3 %collective-permute-start.21 = (bf16[2,128,128]{2,1,0:T(8,128)(2,1)}, bf16[2,128,128]{2,1,0:T(8,128)(2,1)S(1)}, u32[]{:S(2)}, u32[]{:S(2)}) collective-permute-start(bf16[2,128,128]{2,1,0:T(8,128)(2,1)} %next_field.1), channel_id=1, source_target_pairs={{0,4},{4,8},{8,12},{12,0},{1,5},{5,9},{9,13},{13,1},{2,6},{6,10},{... | collective-permute-start | bytes 196616 | tf_op jit(solution)/shard_map/ppermute | solution.py:674
  97.1 6.3 %collective-permute-start.20 = (bf16[2,128,128]{2,1,0:T(8,128)(2,1)}, bf16[2,128,128]{2,1,0:T(8,128)(2,1)S(1)}, u32[]{:S(2)}, u32[]{:S(2)}) collective-permute-start(bf16[2,128,128]{2,1,0:T(8,128)(2,1)} %next_field.1), channel_id=1, source_target_pairs={{0,8},{4,12},{8,0},{12,4},{1,9},{5,13},{9,1},{13,5},{2,10},{6,14},... | collective-permute-start | bytes 196616 | tf_op jit(solution)/shard_map/ppermute | solution.py:674
  97.3 6.7 %collective-permute-start.19 = (bf16[2,128,128]{2,1,0:T(8,128)(2,1)}, bf16[2,128,128]{2,1,0:T(8,128)(2,1)S(1)}, u32[]{:S(2)}, u32[]{:S(2)}) collective-permute-start(bf16[2,128,128]{2,1,0:T(8,128)(2,1)} %next_field.1), channel_id=1, source_target_pairs={{0,12},{4,0},{8,4},{12,8},{1,13},{5,1},{9,5},{13,9},{2,14},{6,2},{... | collective-permute-start | bytes 196616 | tf_op jit(solution)/shard_map/ppermute | solution.py:674
  105.0 8.0 %copy-start.4 = (bf16[8,128,128]{2,1,0:T(8,128)(2,1)}, bf16[8,128,128]{2,1,0:T(8,128)(2,1)S(1)}, u32[]{:S(2)}) copy-start(bf16[8,128,128]{2,1,0:T(8,128)(2,1)S(1)} %constant_dynamic-update-slice_fusion.4.refs_0_) | copy-start | bytes 786436
  105.0 6.4 %collective-permute-start.22 = (bf16[8,128,128]{2,1,0:T(8,128)(2,1)S(1)}, bf16[8,128,128]{2,1,0:T(8,128)(2,1)S(1)}, u32[]{:S(2)}, u32[]{:S(2)}) collective-permute-start(bf16[8,128,128]{2,1,0:T(8,128)(2,1)S(1)} %constant_dynamic-update-slice_fusion.4.refs_0_), channel_id=1, source_target_pairs={{0,2},{1,3},{2,0},{3,1},{4,6},{5,7},{6,4},{7,5},{8,10},{9,11},{10,... | collective-permute-start | bytes 786440 | tf_op jit(solution)/shard_map/ppermute | solution.py:669
  106.3 5.1 %collective-permute-start.23 = (bf16[8,128,128]{2,1,0:T(8,128)(2,1)S(1)}, bf16[8,128,128]{2,1,0:T(8,128)(2,1)S(1)}, u32[]{:S(2)}, u32[]{:S(2)}) collective-permute-start(bf16[8,128,128]{2,1,0:T(8,128)(2,1)S(1)} %constant_dynamic-update-slice_fusion.4.refs_0_), channel_id=1, source_target_pairs={{0,1},{1,0},{2,3},{3,2},{4,5},{5,4},{6,7},{7,6},{8,9},{9,8},{10,11... | collective-permute-start | bytes 786440 | tf_op jit(solution)/shard_map/ppermute | solution.py:666
  111.4 1.5 %copy-start.9 = (bf16[8,128,128]{2,1,0:T(8,128)(2,1)}, bf16[8,128,128]{2,1,0:T(8,128)(2,1)S(1)}, u32[]{:S(2)}) copy-start(bf16[8,128,128]{2,1,0:T(8,128)(2,1)S(1)} %collective-permute-done.22.refs_1_) | copy-start | bytes 786436
  111.4 1.5 %collective-permute-start.24 = (bf16[8,128,128]{2,1,0:T(8,128)(2,1)S(1)}, bf16[8,128,128]{2,1,0:T(8,128)(2,1)S(1)}, u32[]{:S(2)}, u32[]{:S(2)}) collective-permute-start(bf16[8,128,128]{2,1,0:T(8,128)(2,1)S(1)} %collective-permute-done.22.refs_1_), channel_id=1, source_target_pairs={{0,1},{1,0},{2,3},{3,2},{4,5},{5,4},{6,7},{7,6},{8,9},{9,8},{10,11... | collective-permute-start | bytes 786440 | tf_op jit(solution)/shard_map/ppermute | solution.py:666
  111.4 1.5 %copy-start.10 = (bf16[8,128,128]{2,1,0:T(8,128)(2,1)}, bf16[8,128,128]{2,1,0:T(8,128)(2,1)S(1)}, u32[]{:S(2)}) copy-start(bf16[8,128,128]{2,1,0:T(8,128)(2,1)S(1)} %collective-permute-done.23.refs_2_) | copy-start | bytes 786436
  112.9 0.7 copy-start.11
